TPU v7x, 32 devices: a whole 2x2x4 slice. The times are simulated.
32 devices in a mesh: star: 8 (over y, x, core), row: 4 (over z).
Axes of the slice: x: 2, y: 2, z: 4, core: 2. Of those that a mesh axis runs over, the one named last changes fastest.
Arguments:
- feature_maps: bfloat16 [64, 1024, 1024], P(None, 'row'), may hold values from -6 to 6
- coef_table: bfloat16 [64, 64], replicated, may hold values from -0.119628906 to 0.119628906
- star_counts: int32 [8], replicated, may hold values from 1 to 12, 32 in all
- star_cells: int32 [8, 12], replicated, may hold values from 0 to 63
- star_bands: int32 [8, 12], replicated, may hold values from 0 to 7
- psf_cotangent: bfloat16 [96, 1024, 1024], P('star', 'row'), may hold values from -6 to 6
Outputs:
- map_grad: float32 [64, 1024, 1024], P('star', 'row')
- coef_grad: float32 [64, 64], replicated
Inputs may be any that keep to these rules, and one draw needn't show every extreme that they name: The live stars of group g fill its slots 0 to star_counts[g] - 1; the counts sum to 32, and some group has exactly 12.
All inputs are finite; a program needn't handle non-finite values.
Results may differ from a plain program's by a relative error of at most 0.008.
Values may be sent and summed in bfloat16 or wider, within the bound.
A program may use at most 192 MiB of HBM per device.

v0:
```python
import jax
import jax.numpy as jnp
from jax import lax
from jax.sharding import PartitionSpec as P

BANDS = 8
LIVE_DEV = 4


def fourier_tables(pupil_size):
    index_row = jnp.arange(pupil_size, dtype=jnp.int32)
    products = index_row[:, None] * index_row[None, :] % pupil_size
    angles = 2.0 * jnp.pi / pupil_size * products.astype(jnp.float32)
    return (jnp.cos(angles).astype(jnp.bfloat16), (-jnp.sin(angles)).astype(jnp.bfloat16))


def aperture_rows(first_row, row_count, pupil_size):
    centre = 0.5 * (pupil_size - 1)
    row_pos = (first_row + jnp.arange(row_count, dtype=jnp.int32)).astype(jnp.float32) - centre
    col_pos = jnp.arange(pupil_size, dtype=jnp.int32).astype(jnp.float32) - centre
    radius = row_pos[:, None] * row_pos[:, None] + col_pos[None, :] * col_pos[None, :]
    return jnp.where(radius <= 0.25 * pupil_size * pupil_size, 1.0, 0.0).astype(jnp.float32)


def wave_numbers(band_ids):
    wavelength = 0.55 + 0.35 * band_ids.astype(jnp.float32) / (BANDS - 1)
    return 2.0 * jnp.pi / wavelength


def table_pick(values, indices):
    positions = jnp.arange(values.shape[0], dtype=jnp.int32)
    chosen = jnp.where(positions[None, :] == indices[:, None], values[None, :], 0)
    return jnp.sum(chosen, axis=1)


def per_device(feature_maps, coef_table, star_counts, star_cells, star_bands, psf_cotangent):
    groups = lax.axis_size("star")
    my_group = lax.axis_index("star")
    slot_count = psf_cotangent.shape[0]
    map_count, row_count, pupil_size = feature_maps.shape
    group_ends = jnp.cumsum(star_counts)
    group_starts = group_ends - star_counts
    flat_cells = star_cells.reshape(-1)
    flat_bands = star_bands.reshape(-1)
    cell_count = coef_table.shape[0]
    capacity = -(-slot_count // groups)
    targets = jnp.arange(groups, dtype=jnp.int32)
    lane_index = jnp.arange(capacity, dtype=jnp.int32)
    my_start = table_pick(group_starts, my_group[None])
    my_count = table_pick(star_counts, my_group[None])
    first_slot = (targets - my_start) % groups
    send_slot = (first_slot[:, None] + lane_index[None, :] * groups).reshape(-1)
    valid_mask = send_slot < my_count
    picked = jnp.take(psf_cotangent, jnp.minimum(send_slot, slot_count - 1), axis=0)
    outgoing = jnp.where(valid_mask[:, None, None], picked, jnp.zeros_like(picked))
    incoming = lax.all_to_all(outgoing, "star", split_axis=0, concat_axis=0, tiled=True)
    star_rank = my_group + jnp.arange(LIVE_DEV, dtype=jnp.int32) * groups
    owner_group = jnp.sum((group_ends[None, :] <= star_rank[:, None]).astype(jnp.int32), axis=1)
    within = star_rank - table_pick(group_starts, owner_group)
    live_mask = jnp.ones((LIVE_DEV,), dtype=bool)
    owner_group, within, live_mask = (owner_group, within, live_mask)
    cotangent = jnp.take(incoming, owner_group * capacity + within // groups, axis=0)
    slot_index = owner_group * slot_count + within
    cell_ids = table_pick(flat_cells, slot_index)
    band_ids = table_pick(flat_bands, slot_index)
    cell_hot = cell_ids[:, None] == jnp.arange(cell_count, dtype=jnp.int32)[None, :]
    coef_rows = jnp.dot(
        cell_hot.astype(jnp.bfloat16), coef_table, preferred_element_type=jnp.float32
    ).astype(jnp.bfloat16)
    flat_maps = feature_maps.reshape(map_count, row_count * pupil_size)
    path_error = jnp.dot(coef_rows, flat_maps, preferred_element_type=jnp.float32).reshape(
        -1, row_count, pupil_size
    )
    wave_number = wave_numbers(band_ids)
    phase_angle = wave_number[:, None, None] * path_error
    aperture = aperture_rows(lax.axis_index("row") * row_count, row_count, pupil_size)
    cos_phase = jnp.cos(phase_angle)
    sin_phase = jnp.sin(phase_angle)
    pupil_field = jnp.stack([aperture * cos_phase, aperture * sin_phase], 1).astype(jnp.bfloat16)
    cos_table, sin_table = fourier_tables(pupil_size)
    inverse = 1.0 / pupil_size
    along_cos = jnp.einsum(
        "sarc,cv->sarv", pupil_field, cos_table, preferred_element_type=jnp.float32
    )
    along_sin = jnp.einsum(
        "sarc,cv->sarv", pupil_field, sin_table, preferred_element_type=jnp.float32
    )
    column_field = jnp.stack(
        [along_cos[:, 0] - along_sin[:, 1], along_sin[:, 0] + along_cos[:, 1]], 1
    ).astype(jnp.bfloat16)
    pieces = lax.all_to_all(column_field, "row", split_axis=3, concat_axis=2, tiled=True)
    row_cos = jnp.einsum("sarv,ru->savu", pieces, cos_table, preferred_element_type=jnp.float32)
    row_sin = jnp.einsum("sarv,ru->savu", pieces, sin_table, preferred_element_type=jnp.float32)
    real_part = (row_cos[:, 0] - row_sin[:, 1]) * inverse
    imag_part = (row_sin[:, 0] + row_cos[:, 1]) * inverse
    focal_field = jnp.stack([real_part, imag_part], 1)
    weight = jnp.where(live_mask, 2.0, 0.0).astype(jnp.float32)[:, None, None, None]
    focal_grad = (weight * cotangent.astype(jnp.float32)[:, None] * focal_field).astype(
        jnp.bfloat16
    )
    back_cos = jnp.einsum(
        "savu,ur->savr", focal_grad, cos_table, preferred_element_type=jnp.float32
    )
    back_sin = jnp.einsum(
        "savu,ur->savr", focal_grad, sin_table, preferred_element_type=jnp.float32
    )
    spectrum_grad = jnp.stack(
        [(back_cos[:, 0] + back_sin[:, 1]) * inverse, (back_cos[:, 1] - back_sin[:, 0]) * inverse],
        1,
    ).astype(jnp.bfloat16)
    pieces = lax.all_to_all(spectrum_grad, "row", split_axis=3, concat_axis=2, tiled=True)
    col_cos = jnp.einsum("savr,vc->sarc", pieces, cos_table, preferred_element_type=jnp.float32)
    col_sin = jnp.einsum("savr,vc->sarc", pieces, sin_table, preferred_element_type=jnp.float32)
    pupil_grad = jnp.stack([col_cos[:, 0] + col_sin[:, 1], col_cos[:, 1] - col_sin[:, 0]], 1)
    phase_grad = aperture * (cos_phase * pupil_grad[:, 1] - sin_phase * pupil_grad[:, 0])
    path_grad = (
        (wave_number[:, None, None] * phase_grad)
        .astype(jnp.bfloat16)
        .reshape(-1, row_count * pupil_size)
    )
    map_scores = lax.dot_general(
        path_grad, flat_maps, (((1,), (1,)), ((), ())), preferred_element_type=jnp.float32
    )
    coef_part = lax.dot_general(
        cell_hot.astype(jnp.float32),
        map_scores * (1.0 / (8 * pupil_size)),
        (((0,), (0,)), ((), ())),
        precision=lax.Precision.HIGHEST,
    )
    coef_grad = lax.psum(coef_part, ("star", "row"))
    share = map_count // groups
    map_grad = lax.psum_scatter(
        lax.dot_general(
            coef_rows, path_grad, (((0,), (0,)), ((), ())), preferred_element_type=jnp.float32
        ),
        "star",
        scatter_dimension=0,
        tiled=True,
    )
    return (map_grad.reshape(share, row_count, pupil_size), coef_grad)


def solution(mesh):
    placed = (P(None, "row", None), P(), P(), P(), P(), P("star", "row", None))
    return jax.shard_map(
        per_device,
        mesh=mesh,
        in_specs=placed,
        out_specs=(P("star", "row", None), P()),
        check_vma=False,
    )
```

profile of v0, /device:TPU:0, one launch (start us, length us, event | category | flops | bytes accessed | tf_op | source)
XLA Modules:
  0.0 1054.6 jit_solution(7747542769717544505)
XLA Ops:
  7.2 0.8 broadcast_in_dim.115
  8.0 0.8 broadcast_in_dim.118
  8.8 0.8 reduce-window.8
  9.6 1.4 fusion.61
  11.5 0.6 copy-done.14
  12.5 66.2 %fusion = f32[4,256,1024]{2,0,1:T(4,128)} fusion(bf16[4,64]{1,0:T(4,128)(2,1)S(1)} %convolution_convert_fusion, bf16[8,8,256,1024]{3,2,1,0:T(8,128)(2,1)} %bitcast.102), kind=kOutput, calls=%fused_computation.2 | convolution fusion | flops 134217728 | bytes 37749248 | tf_op jit(solution)/shard_map/dot_general | solution.py:71
  78.7 32.4 %fusion.32 = (bf16[4,1,256,1024]{3,0,2,1:T(4,128)(2,1)S(1)}, bf16[4,1,256,1024]{3,0,2,1:T(4,128)(2,1)S(1)}) fusion(f32[4,256,1024]{2,0,1:T(4,128)} %fusion, f32[256,1024]{1,0:T(8,128)S(1)} %fusion.56, f32[4]{0:T(128)S(1)} %add_divide_fusion), kind=kLoop, calls=%fused_computation.59 | loop fusion | flops 5242880 | bytes 9437200 | tf_op jit(solution)/shard_map/stack | solution.py:79
  111.1 3.0 pad_maximum_fusion
  114.1 20.2 %fusion.28 = f32[4,2,256,1024]{3,2,1,0:T(8,128)S(1)} fusion(bf16[4,2,256,1024]{3,0,2,1:T(4,128)(2,1)S(1)} %pad_maximum_fusion), kind=kOutput, calls=%fused_computation.53 | convolution fusion | flops 4311744512 | bytes 12582912 | tf_op jit(solution)/shard_map/sarc,cv->sarv/dot_general | solution.py:85
  134.3 20.0 %fusion.30 = f32[4,2,256,1024]{3,2,1,0:T(8,128)S(1)} fusion(bf16[4,2,256,1024]{3,0,2,1:T(4,128)(2,1)S(1)} %pad_maximum_fusion), kind=kOutput, calls=%fused_computation.55 | convolution fusion | flops 4310695936 | bytes 12582912 | tf_op jit(solution)/shard_map/sarc,cv->sarv/dot_general | solution.py:82
  154.3 1.5 fusion.16
  155.9 2.4 pad_maximum_fusion.1
  158.2 11.2 %copy.43 = bf16[4,2,256,1024]{2,1,0,3:T(2,128)(2,1)} copy(bf16[4,2,256,1024]{3,2,1,0:T(8,128)(2,1)} %pad_maximum_fusion.1) | data formatting | bytes 8388608 | tf_op jit(solution)/shard_map/stack | solution.py:88
  169.4 6.3 all-to-all-start.1
  175.7 0.6 and_select_fusion.1
  176.6 0.8 add_compare_fusion.1
  177.4 7.7 gather_fusion
  185.1 7.8 select_select_fusion
  192.9 76.3 %all-to-all-done.1 = bf16[4,2,256,1024]{2,1,0,3:T(2,128)(2,1)} async-done(((bf16[4,2,256,1024]{2,1,0,3:T(2,128)(2,1)}), bf16[4,2,256,1024]{2,1,0,3:T(2,128)(2,1)}, u32[]{:S(2)}, u32[]{:S(2)}) %all-to-all-start.1) | async-done | bytes 4194336 | tf_op jit(solution)/shard_map/all_to_all | solution.py:91
  269.2 4.9 all-to-all-start
  274.2 7.4 copy.103
  281.6 7.9 all_to_all.33
  289.5 20.3 %fusion.47 = f32[4,2,256,1024]{3,2,1,0:T(8,128)S(1)} fusion(bf16[4,2,1024,256]{2,3,1,0:T(8,128)(2,1)} %all_to_all.33), kind=kOutput, calls=%fused_computation.68 | convolution fusion | flops 4310695936 | bytes 12582912 | tf_op jit(solution)/shard_map/sarv,ru->savu/dot_general | solution.py:92
  309.8 21.1 %fusion.40 = f32[4,2,256,1024]{3,2,1,0:T(8,128)S(1)} fusion(bf16[4,2,1024,256]{2,3,1,0:T(8,128)(2,1)S(1)} %copy-done.6), kind=kOutput, calls=%fused_computation.65 | convolution fusion | flops 4311744512 | bytes 12582912 | tf_op jit(solution)/shard_map/sarv,ru->savu/dot_general | solution.py:93
  331.0 4.6 fusion.14
  335.6 32.6 %all-to-all-done = bf16[16,256,1024]{2,1,0:T(8,128)(2,1)} async-done(((bf16[16,256,1024]{2,1,0:T(8,128)(2,1)}), bf16[16,256,1024]{2,1,0:T(8,128)(2,1)}, u32[]{:S(2)}, u32[]{:S(2)}) %all-to-all-start) | async-done | bytes 8388640 | tf_op jit(solution)/shard_map/all_to_all | solution.py:56
  368.2 4.1 gather_fusion.1
  372.2 0.7 convert_multiply_fusion
  372.9 1.5 copy-done.8
  374.4 20.9 %fusion.38 = f32[4,2,256,1024]{3,2,1,0:T(8,128)S(1)} fusion(f32[4,1,256,1024]{3,2,1,0:T(8,128)} %get-tuple-element.17, f32[4,1,256,1024]{3,2,1,0:T(8,128)S(1)} %copy-done.8, f32[4,256,1024]{2,1,0:T(8,128)S(1)} %convert_multiply_fusion), kind=kOutput, calls=%fused_computation.64 | convolution fusion | flops 4318035968 | bytes 20971520 | tf_op jit(solution)/shard_map/savu,ur->savr/dot_general | solution.py:104
  395.3 20.8 %fusion.45 = f32[4,2,256,1024]{3,2,1,0:T(8,128)S(1)} fusion(f32[4,1,256,1024]{3,2,1,0:T(8,128)} %get-tuple-element.17, f32[4,1,256,1024]{3,2,1,0:T(8,128)S(1)} %copy-done.9, f32[4,256,1024]{2,1,0:T(8,128)S(1)} %convert_multiply_fusion), kind=kOutput, calls=%fused_computation.67 | convolution fusion | flops 4316987392 | bytes 20971520 | tf_op jit(solution)/shard_map/savu,ur->savr/dot_general | solution.py:101
  416.1 2.3 fusion.12
  418.4 2.4 pad_maximum_fusion.2
  420.7 11.2 %copy.45 = bf16[4,2,256,1024]{2,1,0,3:T(2,128)(2,1)} copy(bf16[4,2,256,1024]{3,2,1,0:T(8,128)(2,1)} %pad_maximum_fusion.2) | data formatting | bytes 8388608 | tf_op jit(solution)/shard_map/stack | solution.py:107
  431.9 94.2 %all_to_all.41 = bf16[4,2,256,1024]{2,1,0,3:T(2,128)(2,1)S(1)} all-to-all(bf16[4,2,256,1024]{2,1,0,3:T(2,128)(2,1)} %copy.45), channel_id=1, replica_groups=mesh['star'=8,'row'=4] {'row'}, dimensions={3} | all-to-all | bytes 8388608 | tf_op jit(solution)/shard_map/all_to_all | solution.py:111
  526.1 5.2 copy.102
  531.4 7.7 all_to_all.37
  539.2 22.5 %fusion.36 = f32[4,2,256,1024]{3,2,1,0:T(8,128)} fusion(bf16[4,2,1024,256]{2,3,1,0:T(8,128)(2,1)} %all_to_all.37), kind=kOutput, calls=%fused_computation.63 | convolution fusion | flops 4311744512 | bytes 12582912 | tf_op jit(solution)/shard_map/savr,vc->sarc/dot_general | solution.py:113
  561.7 20.3 %fusion.43 = f32[4,2,256,1024]{3,2,1,0:T(8,128)} fusion(bf16[4,2,1024,256]{2,3,1,0:T(8,128)(2,1)S(1)} %copy-done.7), kind=kOutput, calls=%fused_computation.66 | convolution fusion | flops 4310695936 | bytes 12582912 | tf_op jit(solution)/shard_map/savr,vc->sarc/dot_general | solution.py:112
  581.9 6.9 fusion.100
  589.0 0.3 copy-done.4
  589.3 36.6 %fusion.22 = bf16[4,256,1024]{2,0,1:T(4,128)(2,1)} fusion(f32[4,1,256,1024]{3,2,1,0:T(8,128)S(1)} %get-tuple-element.27, f32[4,1,256,1024]{3,2,1,0:T(8,128)S(1)} %get-tuple-element.21, f32[4,1,256,1024]{3,2,1,0:T(8,128)S(1)} %get-tuple-element.28, f32[4,1,256,1024]{3,2,1,0:T(8,128)S(1)} %get-tuple-element.20, f32[4,256,1024]{2,0,1:T(4,128)S(1)} %copy-done.2, ...), kind=kLoop, calls=%fused_computation.39 | loop fusion | flops 9437184 | bytes 24117264 | tf_op jit(solution)/shard_map/convert_element_type | solution.py:118
  625.9 25.3 %fusion.102 = f32[64,262144]{1,0:T(8,128)} fusion(bf16[4,64]{1,0:T(4,128)(2,1)S(1)} %copy-done.13, bf16[4,262144]{1,0:T(4,128)(2,1)} %bitcast.99), kind=kOutput, calls=%fused_computation.157 | convolution fusion | flops 134217728 | bytes 69206528 | tf_op jit(solution)/shard_map/dot_general | solution.py:133
  651.3 1.6 copy-done.5
  652.8 52.6 %fusion.53 = f32[4,64]{1,0:T(4,128)S(1)} fusion(bf16[4,256,1024]{2,0,1:T(4,128)(2,1)S(1)} %copy-done.5, bf16[64,256,1024]{2,1,0:T(8,128)(2,1)} %param.6), kind=kOutput, calls=%fused_computation.70 | convolution fusion | flops 134217984 | bytes 35652608 | tf_op jit(solution)/shard_map/dot_general | solution.py:121
  705.7 40.7 %psum.7 = f32[64,64]{1,0:T(8,128)} all-reduce(f32[64,64]{1,0:T(8,128)S(1)} %fusion.57), channel_id=1, replica_groups=mesh['star'=8,'row'=4] {'star','row'}, use_global_device_ids=true, to_apply=%region_8.9 | all-reduce | flops 4096 | bytes 32768 | tf_op jit(solution)/shard_map/psum | solution.py:130
  746.4 289.3 %reduce-scatter.2.cloned.1.call-done = f32[8,262144]{1,0:T(8,128)} async-done(((f32[64,262144]{1,0:T(8,128)}), f32[8,262144]{1,0:T(8,128)}) %reduce-scatter.2.cloned.1.call-update) | async-done | bytes 8388624 | tf_op jit(solution)/shard_map/reduce_scatter | solution.py:132
  1035.7 11.6 %copy.52 = f32[8,256,1024]{2,1,0:T(8,128)} copy(f32[8,256,1024]{2,0,1:T(8,128)} %bitcast.98) | data formatting | bytes 16777216
  (52 shorter events, 1.8 us)
Async XLA Ops:
  7.2 4.9 copy-start
  11.5 0.6 copy-start.14
  11.5 67.1 %copy-start.10 = (f32[4]{0:T(128)}, f32[4]{0:T(128)S(1)}, u32[]{:S(2)}) copy-start(f32[4]{0:T(128)S(1)} %add_divide_fusion) | copy-start | bytes 52
  12.3 66.4 %copy-start.12 = (bf16[4,64]{1,0:T(4,128)(2,1)}, bf16[4,64]{1,0:T(4,128)(2,1)S(1)}, u32[]{:S(2)}) copy-start(bf16[4,64]{1,0:T(4,128)(2,1)S(1)} %convolution_convert_fusion) | copy-start | bytes 1540
  12.5 66.2 %copy-start.3 = (f32[256,1024]{1,0:T(8,128)}, f32[256,1024]{1,0:T(8,128)S(1)}, u32[]{:S(2)}) copy-start(f32[256,1024]{1,0:T(8,128)S(1)} %fusion.56) | copy-start | bytes 3145732
  169.4 99.8 %all-to-all-start.1 = ((bf16[4,2,256,1024]{2,1,0,3:T(2,128)(2,1)}), bf16[4,2,256,1024]{2,1,0,3:T(2,128)(2,1)}, u32[]{:S(2)}, u32[]{:S(2)}) async-start(bf16[4,2,256,1024]{2,1,0,3:T(2,128)(2,1)} %copy.43), calls=%async_computation.1 | async-start | bytes 8388608 | tf_op jit(solution)/shard_map/all_to_all | solution.py:91
  269.2 99.0 %all-to-all-start = ((bf16[16,256,1024]{2,1,0:T(8,128)(2,1)}), bf16[16,256,1024]{2,1,0:T(8,128)(2,1)}, u32[]{:S(2)}, u32[]{:S(2)}) async-start(bf16[16,256,1024]{2,1,0:T(8,128)(2,1)} %select_select_fusion), calls=%async_computation | async-start | bytes 16777216 | tf_op jit(solution)/shard_map/all_to_all | solution.py:56
  274.1 761.5 %reduce-scatter.2.cloned.1.call-start = ((), (), s32[]{:S(2)}) async-start(), calls=%async_computation.4 | async-start | bytes 75497472 | tf_op jit(solution)/shard_map/reduce_scatter | solution.py:132
  289.5 20.3 %copy-start.6 = (bf16[4,2,1024,256]{2,3,1,0:T(8,128)(2,1)S(1)}, bf16[4,2,1024,256]{2,3,1,0:T(8,128)(2,1)}, u32[]{:S(2)}) copy-start(bf16[4,2,1024,256]{2,3,1,0:T(8,128)(2,1)} %all_to_all.33) | copy-start | bytes 12582916
  372.2 2.2 copy-start.8
  374.4 20.9 %copy-start.9 = (f32[4,1,256,1024]{3,2,1,0:T(8,128)S(1)}, f32[4,1,256,1024]{3,2,1,0:T(8,128)}, u32[]{:S(2)}) copy-start(f32[4,1,256,1024]{3,2,1,0:T(8,128)} %get-tuple-element.16) | copy-start | bytes 12582916
  539.1 22.5 %copy-start.7 = (bf16[4,2,1024,256]{2,3,1,0:T(8,128)(2,1)S(1)}, bf16[4,2,1024,256]{2,3,1,0:T(8,128)(2,1)}, u32[]{:S(2)}) copy-start(bf16[4,2,1024,256]{2,3,1,0:T(8,128)(2,1)} %all_to_all.37) | copy-start | bytes 12582916
  581.9 7.0 copy-start.2
  581.9 7.3 copy-start.4
  581.9 7.3 copy-start.11
  589.3 36.6 %copy-start.13 = (bf16[4,64]{1,0:T(4,128)(2,1)S(1)}, bf16[4,64]{1,0:T(4,128)(2,1)}, u32[]{:S(2)}) copy-start(bf16[4,64]{1,0:T(4,128)(2,1)} %copy-done.12) | copy-start | bytes 1540
  651.2 1.6 copy-start.5
  652.8 52.6 %copy-start.15 = (s32[4]{0:T(128)S(1)}, s32[4]{0:T(128)}, u32[]{:S(2)}) copy-start(s32[4]{0:T(128)} %copy-done.14) | copy-start | bytes 52
  1035.7 11.7 %copy-start.1 = (bf16[64,64]{1,0:T(8,128)(2,1)S(1)}, bf16[64,64]{1,0:T(8,128)(2,1)}, u32[]{:S(2)}) copy-start(bf16[64,64]{1,0:T(8,128)(2,1)} %param.7) | copy-start | bytes 24580
Sparse Core Ops, SparseCore 0:
  651.4 384.2 reduce-scatter.1
where the time goes:
time: 1070 us; the launch traced here: 1050 us
  waiting for transfers between devices  398 us (37%)
  matrix products  311 us (29%)
  blocking collectives  135 us (13%)
  other arithmetic  98.1 us (9%)
  local copies, waits for them, and re-layouts  86.7 us (8%)
  between operations  14.8 us (1%)
  starting transfers between devices  11.3 us (1%)
    reduce_scatter x1, waiting for transfers between devices, per_device(): lax.psum_scatter(lax.dot_general(coef_rows, path_grad, (((0,), (0,)), (()...  289 us
    all_to_all x1, blocking collectives, per_device(): lax.all_to_all(spectrum_grad, 'row', split_axis=3, concat_axis=2, tiled=T...  94.2 us
    all_to_all x1, waiting for transfers between devices, per_device(): lax.all_to_all(column_field, 'row', split_axis=3, concat_axis=2, tiled=True)  76.3 us
    dot_general x1, matrix products, per_device(): jnp.dot(coef_rows, flat_maps, preferred_element_type=jnp.float32)  66.2 us
    dot_general x1, matrix products, per_device(): lax.dot_general(path_grad, flat_maps, (((1,), (1,)), ((), ())), preferred...  52.6 us
    psum x1, blocking collectives, per_device(): coef_grad = lax.psum(coef_part, ('star', 'row'))  40.7 us
    convert_element_type x1, other arithmetic, per_device(): path_grad = (wave_number[:, None, None] * phase_grad).astype(jnp.bfloat16...  36.6 us
    another operation x2, other arithmetic, per_device(): jnp.stack([aperture * cos_phase, aperture * sin_phase], 1)  35.4 us
  transfers between devices with their start and end apart: 3, of which 3 were waited for; matrix products, arithmetic and copies ran while one was open for 12% of the time, Pallas kernels for 0%

commit v1 on v0

--- a/solution.py
+++ b/solution.py
@@ -1,10 +1,19 @@
+import functools
+
 import jax
 import jax.numpy as jnp
+import numpy as np
 from jax import lax
+from jax.experimental import pallas as pl
+from jax.experimental.pallas import tpu as pltpu
 from jax.sharding import PartitionSpec as P
 
 BANDS = 8
 LIVE_DEV = 4
+RADIX = 4
+ROWS_STEP = 16
+F32 = jnp.float32
+BF16 = jnp.bfloat16
 
 
 def fourier_tables(pupil_size):
@@ -140,10 +149,320 @@
     return (map_grad.reshape(share, row_count, pupil_size), coef_grad)
 
 
+def quarter_tables(size):
+    quarter = size // RADIX
+    place = np.arange(quarter)[None, :, None]
+    freq = RADIX * np.arange(quarter)[None, None, :] + np.arange(RADIX)[:, None, None]
+    angle = 2.0 * np.pi / size * ((place * freq) % size)
+    cosine, sine = np.cos(angle), -np.sin(angle)
+    right = np.concatenate(
+        [np.concatenate([cosine, sine], 2), np.concatenate([-sine, cosine], 2)], 1
+    ).astype(np.float32)
+    left = np.swapaxes(right, 1, 2)
+    return jnp.asarray(right.astype(jnp.bfloat16)), jnp.asarray(left.astype(jnp.bfloat16))
+
+
+def turn_cos_sin(turns):
+    half = turns * np.float32(np.pi)
+    square = half * half
+    sine = jnp.full_like(square, -1.0 / 39916800.0)
+    for term in (1.0 / 362880.0, -1.0 / 5040.0, 1.0 / 120.0, -1.0 / 6.0, 1.0):
+        sine = sine * square + np.float32(term)
+    sine = sine * half
+    cosine = jnp.full_like(square, 1.0 / 479001600.0)
+    for term in (-1.0 / 3628800.0, 1.0 / 40320.0, -1.0 / 720.0, 1.0 / 24.0, -0.5, 1.0):
+        cosine = cosine * square + np.float32(term)
+    return 1.0 - 2.0 * sine * sine, 2.0 * sine * cosine
+
+
+def butterfly(real, imag, sign):
+    sr, dr = real[0] + real[2], real[0] - real[2]
+    si, di = imag[0] + imag[2], imag[0] - imag[2]
+    tr, er = real[1] + real[3], real[1] - real[3]
+    ti, ei = imag[1] + imag[3], imag[1] - imag[3]
+    if sign < 0:
+        er, ei = -er, -ei
+    return (
+        [sr + tr, dr - ei, sr - tr, dr + ei],
+        [si + ti, di + er, si - ti, di - er],
+    )
+
+
+def phase_kernel(inverse_ref, weight_ref, maps_ref, out_ref):
+    stars, rows, size = out_ref.shape
+    maps = maps_ref[...].reshape(maps_ref.shape[0] * rows, size)
+    path = jnp.dot(weight_ref[...], maps, preferred_element_type=F32)
+    for star in range(stars):
+        turns = path[star * rows : (star + 1) * rows] * inverse_ref[star]
+        out_ref[star] = (turns - jnp.floor(turns + 0.5)).astype(BF16)
+
+
+def phase_turns(inverse_wave, coef_rows, feature_maps):
+    map_count, row_count, size = feature_maps.shape
+    stars = coef_rows.shape[0]
+    weights = spread_rows(coef_rows)
+    return pl.pallas_call(
+        phase_kernel,
+        out_shape=jax.ShapeDtypeStruct((stars, row_count, size), BF16),
+        grid=(row_count // ROWS_STEP,),
+        in_specs=[
+            pl.BlockSpec(memory_space=pltpu.SMEM),
+            pl.BlockSpec(weights.shape, lambda i: (0, 0)),
+            pl.BlockSpec((map_count, ROWS_STEP, size), lambda i: (0, i, 0)),
+        ],
+        out_specs=pl.BlockSpec((stars, ROWS_STEP, size), lambda i: (0, i, 0)),
+        cost_estimate=pl.CostEstimate(
+            flops=2 * stars * ROWS_STEP * map_count * row_count * size,
+            bytes_accessed=2 * (map_count + stars) * row_count * size,
+            transcendentals=0,
+        ),
+        compiler_params=pltpu.CompilerParams(vmem_limit_bytes=24 << 20),
+        name="phase_turns",
+    )(inverse_wave, weights, feature_maps)
+
+
+def spread_rows(weights):
+    eye = jnp.eye(ROWS_STEP, dtype=weights.dtype)
+    outs, ins = weights.shape
+    spread = weights[:, None, :, None] * eye[None, :, None, :]
+    return spread.reshape(outs * ROWS_STEP, ins * ROWS_STEP)
+
+
+def star_kernel(
+    chunk, wave_ref, turns_ref, cot_ref, right_ref, left_ref, out_ref, pr, pi, yr, yi, ct, xr, xi
+):
+    size = turns_ref.shape[1]
+    quarter = size // RADIX
+    steps = size // chunk
+    blocks = [slice(m * quarter, (m + 1) * quarter) for m in range(RADIX)]
+    centre = 0.5 * (size - 1)
+    scale = 1.0 / size
+
+    def forward_columns(step, carry):
+        rows = pl.ds(pl.multiple_of(step * chunk, chunk), chunk)
+        cosine, sine = turn_cos_sin(turns_ref[rows, :].astype(F32))
+        row_pos = (
+            lax.broadcasted_iota(jnp.int32, (chunk, size), 0) + step * chunk
+        ).astype(F32) - centre
+        col_pos = lax.broadcasted_iota(jnp.int32, (chunk, size), 1).astype(F32) - centre
+        inside = row_pos * row_pos + col_pos * col_pos <= 0.25 * size * size
+        real = jnp.where(inside, cosine, 0.0)
+        imag = jnp.where(inside, sine, 0.0)
+        pr[rows, :] = real
+        pi[rows, :] = imag
+        mixed_real, mixed_imag = butterfly(
+            [real[:, b] for b in blocks], [imag[:, b] for b in blocks], -1
+        )
+        for k in range(RADIX):
+            both = jnp.concatenate([mixed_real[k].astype(BF16), mixed_imag[k].astype(BF16)], 1)
+            made = jnp.dot(both, right_ref[k], preferred_element_type=F32).astype(BF16)
+            yr[rows, blocks[k]] = made[:, :quarter]
+            yi[rows, blocks[k]] = made[:, quarter:]
+        return carry
+
+    lax.fori_loop(0, steps, forward_columns, 0)
+
+    def pick(k):
+        j = lax.broadcasted_iota(jnp.int32, (quarter, size), 0)
+        f = lax.broadcasted_iota(jnp.int32, (quarter, size), 1)
+        return jnp.where(f == RADIX * j + k, 1.0, 0.0).astype(BF16)
+
+    nt = (((1,), (1,)), ((), ()))
+    for k in range(RADIX):
+        part = lax.dot_general(
+            pick(k), cot_ref[...], nt, preferred_element_type=F32
+        ).astype(BF16)
+        for m in range(RADIX):
+            ct[blocks[k], blocks[m]] = lax.dot_general(
+                part, pick(m), nt, preferred_element_type=F32
+            )
+
+    def focal(step, carry):
+        cols = pl.ds(pl.multiple_of(step * quarter, quarter), quarter)
+        mixed_real, mixed_imag = butterfly(
+            [yr[b, cols].astype(F32) for b in blocks],
+            [yi[b, cols].astype(F32) for b in blocks],
+            -1,
+        )
+        back_real, back_imag = [], []
+        for k in range(RADIX):
+            both = jnp.concatenate([mixed_real[k].astype(BF16), mixed_imag[k].astype(BF16)], 0)
+            field = jnp.dot(left_ref[k], both, preferred_element_type=F32)
+            weight = ct[blocks[k], cols] * (2.0 * scale)
+            grad = (field * jnp.concatenate([weight, weight], 0)).astype(BF16)
+            back = jnp.dot(right_ref[k], grad, preferred_element_type=F32)
+            back_real.append(back[:quarter])
+            back_imag.append(back[quarter:])
+        spec_real, spec_imag = butterfly(back_real, back_imag, 1)
+        for m in range(RADIX):
+            xr[blocks[m], cols] = (spec_real[m] * scale).astype(BF16)
+            xi[blocks[m], cols] = (spec_imag[m] * scale).astype(BF16)
+        return carry
+
+    lax.fori_loop(0, RADIX, focal, 0)
+
+    def inverse_columns(step, carry):
+        rows = pl.ds(pl.multiple_of(step * chunk, chunk), chunk)
+        part_real, part_imag = [], []
+        for k in range(RADIX):
+            both = jnp.concatenate([xr[rows, blocks[k]], xi[rows, blocks[k]]], 1)
+            made = jnp.dot(both, left_ref[k], preferred_element_type=F32)
+            part_real.append(made[:, :quarter])
+            part_imag.append(made[:, quarter:])
+        grad_real, grad_imag = butterfly(part_real, part_imag, 1)
+        wave = wave_ref[0]
+        for m in range(RADIX):
+            grad = pr[rows, blocks[m]] * grad_imag[m] - pi[rows, blocks[m]] * grad_real[m]
+            out_ref[rows, blocks[m]] = (wave * grad).astype(BF16)
+        return carry
+
+    lax.fori_loop(0, steps, inverse_columns, 0)
+
+
+def star_gradient(wave, turns, cotangent, right, left):
+    size = turns.shape[0]
+    vmem = pl.BlockSpec(memory_space=pltpu.VMEM)
+    square = (size, size)
+    return pl.pallas_call(
+        functools.partial(star_kernel, 128),
+        out_shape=jax.ShapeDtypeStruct(square, BF16),
+        in_specs=[pl.BlockSpec(memory_space=pltpu.SMEM), vmem, vmem, vmem, vmem],
+        out_specs=vmem,
+        scratch_shapes=[
+            pltpu.VMEM(square, F32),
+            pltpu.VMEM(square, F32),
+            pltpu.VMEM(square, BF16),
+            pltpu.VMEM(square, BF16),
+            pltpu.VMEM(square, F32),
+            pltpu.VMEM(square, BF16),
+            pltpu.VMEM(square, BF16),
+        ],
+        compiler_params=pltpu.CompilerParams(vmem_limit_bytes=56 << 20),
+        name="star_gradient",
+    )(wave, turns, cotangent, right, left)
+
+
+def maps_kernel(group_ref, weight_ref, grad_ref, maps_ref, out_ref, score_ref):
+    share, rows, size = out_ref.shape
+    grads = grad_ref[...].reshape(grad_ref.shape[0] * rows, size)
+    maps = maps_ref[...].reshape(share * rows, size)
+    total = jnp.dot(weight_ref[...], grads, preferred_element_type=F32)
+    out_ref[...] = total.reshape(share, rows, size)
+
+    @pl.when(pl.program_id(0) == 0)
+    def _():
+        score_ref[...] = jnp.zeros_like(score_ref)
+
+    score_ref[...] += lax.dot_general(
+        maps, grads, (((1,), (1,)), ((), ())), preferred_element_type=F32
+    )
+
+
+def map_sums(my_group, coef_rows, path_grads, feature_maps, share):
+    stars, row_count, size = path_grads.shape
+    weights = spread_rows(coef_rows)
+    score_shape = (share * ROWS_STEP, stars * ROWS_STEP)
+    map_grad, scores = pl.pallas_call(
+        maps_kernel,
+        out_shape=(
+            jax.ShapeDtypeStruct((share, row_count, size), F32),
+            jax.ShapeDtypeStruct(score_shape, F32),
+        ),
+        grid_spec=pltpu.PrefetchScalarGridSpec(
+            num_scalar_prefetch=1,
+            grid=(row_count // ROWS_STEP,),
+            in_specs=[
+                pl.BlockSpec(weights.shape, lambda i, g: (0, 0)),
+                pl.BlockSpec((stars, ROWS_STEP, size), lambda i, g: (0, i, 0)),
+                pl.BlockSpec((share, ROWS_STEP, size), lambda i, g: (g[0], i, 0)),
+            ],
+            out_specs=(
+                pl.BlockSpec((share, ROWS_STEP, size), lambda i, g: (0, i, 0)),
+                pl.BlockSpec(score_shape, lambda i, g: (0, 0)),
+            ),
+        ),
+        compiler_params=pltpu.CompilerParams(vmem_limit_bytes=24 << 20),
+        name="map_sums",
+    )(my_group[None], weights, path_grads, feature_maps)
+    eye = jnp.eye(ROWS_STEP, dtype=F32)
+    scores = scores.reshape(share, ROWS_STEP, stars, ROWS_STEP)
+    return map_grad, jnp.sum(scores * eye[None, :, None, :], axis=(1, 3))
+
+
+def star_devices(feature_maps, coef_table, star_counts, star_cells, star_bands, psf_cotangent):
+    groups = lax.axis_size("star")
+    lanes = lax.axis_size("row")
+    my_group = lax.axis_index("star")
+    my_lane = lax.axis_index("row")
+    slot_count = psf_cotangent.shape[0]
+    map_count, row_count, size = feature_maps.shape
+    cell_count = coef_table.shape[0]
+    share = map_count // groups
+    group_ends = jnp.cumsum(star_counts)
+    group_starts = group_ends - star_counts
+    capacity = -(-slot_count // groups)
+    targets = jnp.arange(groups, dtype=jnp.int32)
+    my_start = table_pick(group_starts, my_group[None])
+    first_slot = (targets - my_start) % groups
+    lane_index = jnp.arange(capacity, dtype=jnp.int32)
+    send_slot = (first_slot[:, None] + lane_index[None, :] * groups).reshape(-1)
+    outgoing = jnp.take(
+        psf_cotangent, jnp.minimum(send_slot, slot_count - 1), axis=0, mode="clip"
+    )
+    incoming = lax.all_to_all(outgoing, "star", split_axis=0, concat_axis=0, tiled=True)
+
+    total = groups * lanes
+    order = jnp.arange(total, dtype=jnp.int32)
+    rank = order // lanes + (order % lanes) * groups
+    owner = jnp.sum((group_ends[None, :] <= rank[:, None]).astype(jnp.int32), axis=1)
+    within = rank - table_pick(group_starts, owner)
+    slot_index = owner * slot_count + within
+    cell_ids = table_pick(star_cells.reshape(-1), slot_index)
+    band_ids = table_pick(star_bands.reshape(-1), slot_index)
+    cell_hot = cell_ids[:, None] == jnp.arange(cell_count, dtype=jnp.int32)[None, :]
+    coef_rows = jnp.dot(
+        cell_hot.astype(BF16), coef_table, preferred_element_type=F32
+    ).astype(BF16)
+
+    def mine(values):
+        return lax.dynamic_slice_in_dim(values, my_group * lanes, lanes, 0)
+
+    wavelength = 0.55 + 0.35 * band_ids.astype(F32) / (BANDS - 1)
+    turns = phase_turns(mine(1.0 / wavelength), mine(coef_rows), feature_maps)
+    turns = lax.all_to_all(turns, "row", split_axis=0, concat_axis=0, tiled=True)
+    cotangent = jnp.take(
+        incoming, mine(owner) * capacity + mine(within) // groups, axis=0, mode="clip"
+    )
+    cotangent = lax.all_to_all(cotangent, "row", split_axis=0, concat_axis=0, tiled=True)
+    wave = wave_numbers(band_ids)
+    my_wave = lax.dynamic_slice_in_dim(wave, my_group * lanes + my_lane, 1, 0)
+    right, left = quarter_tables(size)
+    path_grad = star_gradient(
+        my_wave, turns.reshape(size, size), cotangent.reshape(size, size), right, left
+    )
+    path_grad = lax.all_to_all(
+        path_grad.reshape(lanes, row_count, size), "row", split_axis=0, concat_axis=0, tiled=True
+    )
+    path_grads = lax.all_gather(path_grad, "star", axis=0, tiled=True)
+    my_coefs = lax.dynamic_slice_in_dim(coef_rows.T, my_group * share, share, 0)
+    map_grad, scores = map_sums(my_group, my_coefs, path_grads, feature_maps, share)
+    coef_part = lax.dot_general(
+        cell_hot.astype(F32),
+        scores * (1.0 / (8 * size)),
+        (((0,), (1,)), ((), ())),
+        precision=lax.Precision.HIGHEST,
+    )
+    placed = lax.dynamic_update_slice_in_dim(
+        jnp.zeros((cell_count, map_count), F32), coef_part, my_group * share, 1
+    )
+    return map_grad, lax.psum(placed, ("star", "row"))
+
+
 def solution(mesh):
     placed = (P(None, "row", None), P(), P(), P(), P(), P("star", "row", None))
+    device = star_devices if mesh.shape["row"] == LIVE_DEV else per_device
     return jax.shard_map(
-        per_device,
+        device,
         mesh=mesh,
         in_specs=placed,
         out_specs=(P("star", "row", None), P()),

time: 1070 us -> 467 us (0.44); the launches traced: 1050 us -> 466 us
  matrix products: 311 us -> 0.47 us
  waiting for transfers between devices: 398 us -> 247 us
  other arithmetic: 98.1 us -> 3.94 us
  Pallas kernels: 0 us -> 66.7 us
  local copies, waits for them, and re-layouts: 86.7 us -> 25.9 us
  blocking collectives: 135 us -> 92.3 us
    dot_general x13 -> x2, matrix products: 311 us -> 0.47 us  [the longest x1 0.28 us: star_devices(): lax.dot_general(cell_hot.astype(F32), scores * (1.0 / (8 * size)), (((0,)...]
    reduce_scatter x1 -> x0, waiting for transfers between devices: 289 us -> none  [per_device(): lax.psum_scatter(lax.dot_general(coef_rows, path_grad, (((0,), (0,)), (()...]
    all_gather x0 -> x1, waiting for transfers between devices: none -> 88.1 us  [star_devices(): path_grads = lax.all_gather(path_grad, 'star', axis=0, tiled=True)]
    pallas_call x0 -> x3, Pallas kernels: none -> 66.7 us  [the longest x1 29.7 us: star_gradient(): pl.pallas_call(functools.partial(star_kernel, 128), out_shape=jax.ShapeDt...]
    all_to_all x2 -> x3, waiting for transfers between devices: 109 us -> 159 us  [the longest x1 72 us: star_devices(): lax.all_to_all(outgoing, 'star', split_axis=0, concat_axis=0, tiled=True)]
    another operation x7 -> x1, other arithmetic: 44.8 us -> 0.83 us  [the longest x2 35.4 us: per_device(): jnp.stack([aperture * cos_phase, aperture * sin_phase], 1)]
    all_to_all x1, blocking collectives: 94.2 us -> 52.2 us  [star_devices(): lax.all_to_all(path_grad.reshape(lanes, row_count, size), 'row', split_ax...]
    convert_element_type x1 -> x2, other arithmetic: 36.6 us -> 0.01 us  [the longest x1 0.01 us: spread_rows(): eye = jnp.eye(ROWS_STEP, dtype=weights.dtype)]
  transfers between devices with their start and end apart: 3 -> 4, of which waited for: 3 -> 4; matrix products, arithmetic and copies ran while one was open for 12% -> 2% of each run, Pallas kernels for 0% -> 4%
where the time goes in v1:
time: 467 us; the launch traced here: 466 us
  waiting for transfers between devices  247 us (53%)
  blocking collectives  92.3 us (20%)
  Pallas kernels  66.7 us (14%)
  local copies, waits for them, and re-layouts  25.9 us (6%)
  starting transfers between devices  15.5 us (3%)
  between operations  14.2 us (3%)
    all_gather x1, waiting for transfers between devices, star_devices(): path_grads = lax.all_gather(path_grad, 'star', axis=0, tiled=True)  88.1 us
    all_to_all x1, waiting for transfers between devices, star_devices(): lax.all_to_all(outgoing, 'star', split_axis=0, concat_axis=0, tiled=True)  72 us
    all_to_all x1, blocking collectives, star_devices(): lax.all_to_all(path_grad.reshape(lanes, row_count, size), 'row', split_ax...  52.2 us
    all_to_all x1, waiting for transfers between devices, star_devices(): lax.all_to_all(cotangent, 'row', split_axis=0, concat_axis=0, tiled=True)  47.2 us
    psum x1, blocking collectives, star_devices(): return (map_grad, lax.psum(placed, ('star', 'row')))  40.1 us
    all_to_all x1, waiting for transfers between devices, star_devices(): lax.all_to_all(turns, 'row', split_axis=0, concat_axis=0, tiled=True)  39.7 us
    pallas_call x1, Pallas kernels, star_gradient(): pl.pallas_call(functools.partial(star_kernel, 128), out_shape=jax.ShapeDt...  29.7 us
    pallas_call x1, Pallas kernels, phase_turns(): pl.pallas_call(phase_kernel, out_shape=jax.ShapeDtypeStruct((stars, row_c...  19.7 us
  transfers between devices with their start and end apart: 4, of which 4 were waited for; matrix products, arithmetic and copies ran while one was open for 2% of the time, Pallas kernels for 4%

profile of v1, /device:TPU:0, one launch (start us, length us, event | category | flops | bytes accessed | tf_op | source)
XLA Modules:
  0.0 466.0 jit_solution(1825013332384396487)
XLA Ops:
  7.2 0.0 copy-start
  7.2 0.8 reduce-window.8
  8.0 1.3 fusion.11
  9.3 0.7 and_select_fusion.1
  10.0 0.1 add_minimum_fusion
  10.1 0.1 reshape.160
  10.1 7.7 %gather_fusion = bf16[16,256,1024]{2,1,0:T(8,128)(2,1)} fusion(bf16[12,256,1024]{2,1,0:T(8,128)(2,1)} %param.13, s32[1024]{0:T(1024)S(1)} %pad_clamp_fusion.1), kind=kCustom, calls=%fused_computation | custom fusion | bytes 16777280 | tf_op jit(solution)/shard_map/jit(_take)/gather | solution.py:409
  17.8 0.0 copy-start.4
  17.8 5.3 %all-to-all-start.1 = ((bf16[16,256,1024]{2,1,0:T(8,128)(2,1)}), bf16[16,256,1024]{2,1,0:T(8,128)(2,1)}, u32[]{:S(2)}, u32[]{:S(2)}) async-start(bf16[16,256,1024]{2,1,0:T(8,128)(2,1)} %gather_fusion), calls=%async_computation.1 | async-start | bytes 16777216 | tf_op jit(solution)/shard_map/all_to_all | solution.py:412
  23.2 0.0 copy-done.4
  23.2 0.1 broadcast_in_dim.73
  23.3 0.0 copy-done.5
  23.3 0.1 broadcast_in_dim.76
  23.3 0.1 convert_reduce_fusion
  23.4 0.1 select_reduce_fusion.2
  23.5 0.2 select_reduce_fusion
  23.7 0.0 copy-done
  23.7 0.2 convolution_convert_fusion
  23.9 0.1 broadcast_multiply_fusion
  24.1 1.8 mul.110.weight_ref
  25.9 0.1 dynamic_slice.20.inverse_ref
  25.9 19.7 %phase_turns.1 = bf16[4,256,1024]{2,1,0:T(8,128)(2,1)} custom-call(f32[4]{0:T(128)S(1)} %dynamic_slice.20.inverse_ref, bf16[64,1024]{1,0:T(8,128)(2,1)S(1)} %mul.110.weight_ref, bf16[64,256,1024]{2,1,0:T(8,128)(2,1)} %maps_ref.3), custom_call_target="tpu_custom_call" | custom-call | flops 2147483648 | bytes 35651584 | tf_op jit(solution)/shard_map/phase_turns/pallas_call | solution.py:204
  45.6 72.0 %all-to-all-done.1 = bf16[16,256,1024]{2,1,0:T(8,128)(2,1)} async-done(((bf16[16,256,1024]{2,1,0:T(8,128)(2,1)}), bf16[16,256,1024]{2,1,0:T(8,128)(2,1)}, u32[]{:S(2)}, u32[]{:S(2)}) %all-to-all-start.1) | async-done | bytes 8388640 | tf_op jit(solution)/shard_map/all_to_all | solution.py:412
  117.7 5.7 %all-to-all-start = ((bf16[4,256,1024]{2,1,0:T(8,128)(2,1)}), bf16[4,256,1024]{2,1,0:T(8,128)(2,1)S(1)}, u32[]{:S(2)}, u32[]{:S(2)}) async-start(bf16[4,256,1024]{2,1,0:T(8,128)(2,1)} %phase_turns.1), calls=%async_computation | async-start | bytes 4194304 | tf_op jit(solution)/shard_map/all_to_all | solution.py:432
  123.3 0.1 fusion.13
  123.4 5.5 %gather_fusion.1 = bf16[4,256,1024]{2,1,0:T(8,128)(2,1)} fusion(bf16[16,256,1024]{2,1,0:T(8,128)(2,1)} %all-to-all-done.1, s32[1024]{0:T(1024)S(1)} %pad_clamp_fusion), kind=kCustom, calls=%fused_computation.1 | custom fusion | bytes 4194320 | tf_op jit(solution)/shard_map/jit(_take)/gather | solution.py:433
  128.9 39.7 %all-to-all-done = bf16[4,256,1024]{2,1,0:T(8,128)(2,1)S(1)} async-done(((bf16[4,256,1024]{2,1,0:T(8,128)(2,1)}), bf16[4,256,1024]{2,1,0:T(8,128)(2,1)S(1)}, u32[]{:S(2)}, u32[]{:S(2)}) %all-to-all-start) | async-done | bytes 2097184 | tf_op jit(solution)/shard_map/all_to_all | solution.py:432
  168.6 1.3 copy-done.3
  169.9 4.4 all-to-all-start.2
  174.3 0.0 all-gather.2.cloned.1.call-start
  174.4 0.6 dynamic_slice.19.wave_ref
  175.0 47.2 %all-to-all-done.2 = bf16[4,256,1024]{2,1,0:T(8,128)(2,1)} async-done(((bf16[4,256,1024]{2,1,0:T(8,128)(2,1)}), bf16[4,256,1024]{2,1,0:T(8,128)(2,1)}, u32[]{:S(2)}, u32[]{:S(2)}) %all-to-all-start.2) | async-done | bytes 2097184 | tf_op jit(solution)/shard_map/all_to_all | solution.py:436
  222.2 29.7 %star_gradient.1 = bf16[1024,1024]{1,0:T(8,128)(2,1)} custom-call(f32[1]{0:T(128)} %dynamic_slice.19.wave_ref, bf16[1024,1024]{1,0:T(8,128)(2,1)} %bitcast.15, bf16[1024,1024]{1,0:T(8,128)(2,1)} %bitcast.5.cot_ref, bf16[4,512,512]{2,1,0:T(8,128)(2,1)} %constant.106.clone.right_ref, bf16[4,512,512]{2,1,0:T(8,128)(2,1)} %constant.107.clone.left_ref), custom_call_target="tpu_custom_call" | custom-call | tf_op jit(solution)/shard_map/star_gradient/pallas_call | solution.py:326
  251.9 52.2 %all_to_all.20 = bf16[4,256,1024]{2,1,0:T(8,128)(2,1)} all-to-all(bf16[4,256,1024]{2,1,0:T(8,128)(2,1)} %bitcast.16), channel_id=1, replica_groups=mesh['star'=8,'row'=4] {'row'}, dimensions={0} | all-to-all | bytes 4194304 | tf_op jit(solution)/shard_map/all_to_all | solution.py:443
  304.1 0.0 all-gather.2.cloned.1.call-update
  304.1 0.1 dynamic-slice_bitcast_fusion
  304.2 0.1 copy.16
  304.3 0.1 broadcast_multiply_fusion.1
  304.4 1.8 mul.105.weight_ref
  306.2 88.1 %all-gather.2.cloned.1.call-done.grad_ref = bf16[32,256,1024]{2,1,0:T(8,128)(2,1)} async-done(((bf16[4,256,1024]{2,1,0:T(8,128)(2,1)}), bf16[32,256,1024]{2,1,0:T(8,128)(2,1)}) %all-gather.2.cloned.1.call-update) | async-done | bytes 16777232 | tf_op jit(solution)/shard_map/all_gather | solution.py:446
  394.3 5.8 %copy-done.2 = bf16[32,256,1024]{2,1,0:T(8,128)(2,1)S(1)} copy-done((bf16[32,256,1024]{2,1,0:T(8,128)(2,1)S(1)}, bf16[32,256,1024]{2,1,0:T(8,128)(2,1)}, u32[]{:S(2)}) %copy-start.2) | copy-done | bytes 16777240
  400.1 17.3 %map_sums.1 = (f32[8,256,1024]{2,1,0:T(8,128)}, f32[128,512]{1,0:T(8,128)S(1)}) custom-call(s32[1]{0:T(128)} %bitcast.group_ref, bf16[128,512]{1,0:T(8,128)(2,1)S(1)} %mul.105.weight_ref, bf16[32,256,1024]{2,1,0:T(8,128)(2,1)S(1)} %copy-done.2, bf16[64,256,1024]{2,1,0:T(8,128)(2,1)} %maps_ref.3), custom_call_target="tpu_custom_call" | custom-call | tf_op jit(solution)/shard_map/map_sums/pallas_call | solution.py:365
  417.3 0.7 reshape.157
  418.1 0.3 multiply_reduce_fusion
  418.4 0.3 fusion.1
  418.7 0.3 dynamic_update_slice.3
  419.0 40.1 %psum.7 = f32[64,64]{1,0:T(8,128)} all-reduce(f32[64,64]{1,0:T(8,128)S(1)} %dynamic_update_slice.3), channel_id=1, replica_groups=mesh['star'=8,'row'=4] {'star','row'}, use_global_device_ids=true, to_apply=%region_7.8 | all-reduce | flops 4096 | bytes 32768 | tf_op jit(solution)/shard_map/psum | solution.py:458
  459.1 0.0 copy-done.1
  (14 shorter events, 0.1 us)
Async XLA Ops:
  7.2 16.5 %copy-start = (bf16[64,64]{1,0:T(8,128)(2,1)S(1)}, bf16[64,64]{1,0:T(8,128)(2,1)}, u32[]{:S(2)}) copy-start(bf16[64,64]{1,0:T(8,128)(2,1)} %param.9) | copy-start | bytes 24580
  17.8 5.3 %copy-start.4 = (s32[8,12]{1,0:T(8,128)S(1)}, s32[8,12]{1,0:T(8,128)}, u32[]{:S(2)}) copy-start(s32[8,12]{1,0:T(8,128)} %param.11) | copy-start | bytes 1156
  17.8 5.4 %copy-start.5 = (s32[8,12]{1,0:T(8,128)S(1)}, s32[8,12]{1,0:T(8,128)}, u32[]{:S(2)}) copy-start(s32[8,12]{1,0:T(8,128)} %param.12) | copy-start | bytes 1156
  17.8 99.8 %all-to-all-start.1 = ((bf16[16,256,1024]{2,1,0:T(8,128)(2,1)}), bf16[16,256,1024]{2,1,0:T(8,128)(2,1)}, u32[]{:S(2)}, u32[]{:S(2)}) async-start(bf16[16,256,1024]{2,1,0:T(8,128)(2,1)} %gather_fusion), calls=%async_computation.1 | async-start | bytes 16777216 | tf_op jit(solution)/shard_map/all_to_all | solution.py:412
  117.7 50.9 %all-to-all-start = ((bf16[4,256,1024]{2,1,0:T(8,128)(2,1)}), bf16[4,256,1024]{2,1,0:T(8,128)(2,1)S(1)}, u32[]{:S(2)}, u32[]{:S(2)}) async-start(bf16[4,256,1024]{2,1,0:T(8,128)(2,1)} %phase_turns.1), calls=%async_computation | async-start | bytes 4194304 | tf_op jit(solution)/shard_map/all_to_all | solution.py:432
  168.6 1.3 copy-start.3
  169.9 52.3 %all-to-all-start.2 = ((bf16[4,256,1024]{2,1,0:T(8,128)(2,1)}), bf16[4,256,1024]{2,1,0:T(8,128)(2,1)}, u32[]{:S(2)}, u32[]{:S(2)}) async-start(bf16[4,256,1024]{2,1,0:T(8,128)(2,1)} %gather_fusion.1), calls=%async_computation.2 | async-start | bytes 4194304 | tf_op jit(solution)/shard_map/all_to_all | solution.py:436
  174.3 220.0 %all-gather.2.cloned.1.call-start = ((), (), s32[]{:S(2)}) async-start(), calls=%async_computation.4 | async-start | bytes 18874368 | tf_op jit(solution)/shard_map/all_gather | solution.py:446
  394.3 5.8 %copy-start.2 = (bf16[32,256,1024]{2,1,0:T(8,128)(2,1)S(1)}, bf16[32,256,1024]{2,1,0:T(8,128)(2,1)}, u32[]{:S(2)}) copy-start(bf16[32,256,1024]{2,1,0:T(8,128)(2,1)} %all-gather.2.cloned.1.call-done.grad_ref) | copy-start | bytes 50331652
  417.3 41.8 %copy-start.1 = (bf16[64,64]{1,0:T(8,128)(2,1)S(1)}, bf16[64,64]{1,0:T(8,128)(2,1)}, u32[]{:S(2)}) copy-start(bf16[64,64]{1,0:T(8,128)(2,1)} %param.9) | copy-start | bytes 24580
Sparse Core Ops, SparseCore 0:
  304.2 90.0 all-gather.1

commit v2 on v1

--- a/solution.py
+++ b/solution.py
@@ -10,6 +10,7 @@
 
 BANDS = 8
 LIVE_DEV = 4
+PLANE_DEV = 8
 RADIX = 4
 ROWS_STEP = 16
 F32 = jnp.float32
@@ -389,6 +390,225 @@
     return map_grad, jnp.sum(scores * eye[None, :, None, :], axis=(1, 3))
 
 
+GATHER_STEPS = 8
+
+
+def greet(peers):
+    barrier = pltpu.get_barrier_semaphore()
+    for peer in peers:
+        pl.semaphore_signal(barrier, inc=1, device_id=peer, device_id_type=pl.DeviceIdType.MESH)
+    pl.semaphore_wait(barrier, len(peers))
+
+
+def send(source, target, send_sem, recv_sem, peer):
+    return pltpu.make_async_remote_copy(
+        src_ref=source,
+        dst_ref=target,
+        send_sem=send_sem,
+        recv_sem=recv_sem,
+        device_id=peer,
+        device_id_type=pl.DeviceIdType.MESH,
+    )
+
+
+def row_kernel(lanes, in_ref, out_ref, local_sem, send_sem, recv_sem):
+    row = lax.axis_index("row")
+    peers = [{"row": (row + d) % lanes} for d in range(1, lanes)]
+    greet(peers)
+    copies = [
+        send(
+            in_ref.at[(row + d) % lanes],
+            out_ref.at[row],
+            send_sem.at[d - 1],
+            recv_sem.at[d - 1],
+            peers[d - 1],
+        )
+        for d in range(1, lanes)
+    ]
+    for copy in copies:
+        copy.start()
+    own = pltpu.make_async_copy(in_ref.at[row], out_ref.at[row], local_sem)
+    own.start()
+    own.wait()
+    for copy in copies:
+        copy.wait()
+
+
+def row_exchange(blocks, collective_id):
+    lanes = blocks.shape[0]
+    return pl.pallas_call(
+        functools.partial(row_kernel, lanes),
+        out_shape=jax.ShapeDtypeStruct(blocks.shape, blocks.dtype),
+        in_specs=[pl.BlockSpec(memory_space=pltpu.VMEM)],
+        out_specs=pl.BlockSpec(memory_space=pl.ANY),
+        scratch_shapes=[
+            pltpu.SemaphoreType.DMA,
+            pltpu.SemaphoreType.DMA((lanes - 1,)),
+            pltpu.SemaphoreType.DMA((lanes - 1,)),
+        ],
+        compiler_params=pltpu.CompilerParams(
+            collective_id=collective_id, has_side_effects=True, vmem_limit_bytes=8 << 20
+        ),
+        cost_estimate=pl.CostEstimate(
+            flops=0, bytes_accessed=50 * blocks.size * 2, transcendentals=0
+        ),
+        name="row_exchange",
+    )(blocks)
+
+
+def gather_kernel(lanes, in_ref, out_ref, local, z_send, z_recv, p_send, p_recv, c_send, c_recv):
+    row = lax.axis_index("row")
+    me = lax.axis_index("star")
+    depth = in_ref.shape[1] // GATHER_STEPS
+    core = me + 1 - 2 * (me % 2)
+    across = me + 2 - 4 * ((me // 2) % 2)
+    along = me + 4 - 8 * ((me // 4) % 2)
+    corner = across + 4 - 8 * ((me // 4) % 2)
+    peers = [{"row": (row + d) % lanes} for d in range(1, lanes)]
+    to_core, to_across, to_along = {"star": core}, {"star": across}, {"star": along}
+    greet(peers + [to_core, to_across, to_along])
+    half = lanes // 2
+    started = []
+
+    def start(copy):
+        copy.start()
+        started.append(copy)
+        return copy
+
+    def block(group, step, first=0, count=lanes):
+        return out_ref.at[group, pl.ds(first, count), pl.ds(step * depth, depth)]
+
+    own, exchanged = [], []
+    for step in range(GATHER_STEPS):
+        rows = pl.ds(step * depth, depth)
+        copy = pltpu.make_async_copy(
+            in_ref.at[row, rows], out_ref.at[me, row, rows], local.at[step]
+        )
+        copy.start()
+        own.append(copy)
+        exchanged.append(
+            [
+                start(
+                    send(
+                        in_ref.at[(row + d) % lanes, rows],
+                        out_ref.at[me, row, rows],
+                        z_send.at[step, d - 1],
+                        z_recv.at[step, d - 1],
+                        peers[d - 1],
+                    )
+                )
+                for d in range(1, lanes)
+            ]
+        )
+
+    def plane(step, way, part, peer):
+        return start(send(part, part, p_send.at[step, way], p_recv.at[step, way], peer))
+
+    def cores(step, way, part):
+        return start(send(part, part, c_send.at[step, way], c_recv.at[step, way], to_core))
+
+    sides, corners, twins = {}, {}, []
+    for step in range(GATHER_STEPS + 2):
+        if step < GATHER_STEPS:
+            own[step].wait()
+            for copy in exchanged[step]:
+                copy.wait_recv()
+            part = block(me, step)
+            sides[step] = (
+                plane(step, 0, part, to_across),
+                plane(step, 1, part, to_along),
+            )
+            twins.append(cores(step, 0, part))
+        last = step - 1
+        if 0 <= last < GATHER_STEPS:
+            sides[last][0].wait_recv()
+            first = plane(last, 2, block(across, last, 0, half), to_along)
+            twins.append(cores(last, 1, block(across, last)))
+            sides[last][1].wait_recv()
+            second = plane(last, 3, block(along, last, half, lanes - half), to_across)
+            twins.append(cores(last, 2, block(along, last)))
+            corners[last] = (first, second)
+        last = step - 2
+        if last >= 0:
+            corners[last][0].wait_recv()
+            corners[last][1].wait_recv()
+            twins.append(cores(last, 3, block(corner, last)))
+    for copy in twins:
+        copy.wait_recv()
+    for copy in started:
+        copy.wait_send()
+
+
+def gather_grads(path_grad, groups):
+    lanes, row_count, size = path_grad.shape
+    dma = pltpu.SemaphoreType.DMA
+    return pl.pallas_call(
+        functools.partial(gather_kernel, lanes),
+        out_shape=jax.ShapeDtypeStruct((groups, lanes, row_count, size), path_grad.dtype),
+        in_specs=[pl.BlockSpec(memory_space=pltpu.VMEM)],
+        out_specs=pl.BlockSpec(memory_space=pl.ANY),
+        scratch_shapes=[
+            dma((GATHER_STEPS,)),
+            dma((GATHER_STEPS, lanes - 1)),
+            dma((GATHER_STEPS, lanes - 1)),
+            dma((GATHER_STEPS, 4)),
+            dma((GATHER_STEPS, 4)),
+            dma((GATHER_STEPS, 4)),
+            dma((GATHER_STEPS, 4)),
+        ],
+        compiler_params=pltpu.CompilerParams(
+            collective_id=1, has_side_effects=True, vmem_limit_bytes=8 << 20
+        ),
+        name="gather_grads",
+    )(path_grad)
+
+
+def score_kernel(groups, lanes, in_ref, out_ref, z_send, z_recv, s_send, s_recv):
+    row = lax.axis_index("row")
+    me = lax.axis_index("star")
+    row_peers = [{"row": (row + d) % lanes} for d in range(1, lanes)]
+    star_peers = [{"star": (me + d) % groups} for d in range(1, groups)]
+    greet(row_peers + star_peers)
+    copies = [
+        send(in_ref, out_ref.at[me, row], z_send.at[d], z_recv.at[d], row_peers[d])
+        for d in range(lanes - 1)
+    ]
+    for copy in copies:
+        copy.start()
+    out_ref[me, row] = in_ref[...]
+    for copy in copies:
+        copy.wait()
+    copies = [
+        send(out_ref.at[me], out_ref.at[me], s_send.at[d], s_recv.at[d], star_peers[d])
+        for d in range(groups - 1)
+    ]
+    for copy in copies:
+        copy.start()
+    for copy in copies:
+        copy.wait()
+
+
+def gather_scores(scores, groups, lanes):
+    dma = pltpu.SemaphoreType.DMA
+    vmem = pl.BlockSpec(memory_space=pltpu.VMEM)
+    return pl.pallas_call(
+        functools.partial(score_kernel, groups, lanes),
+        out_shape=jax.ShapeDtypeStruct((groups, lanes) + scores.shape, scores.dtype),
+        in_specs=[vmem],
+        out_specs=vmem,
+        scratch_shapes=[
+            dma((lanes - 1,)),
+            dma((lanes - 1,)),
+            dma((groups - 1,)),
+            dma((groups - 1,)),
+        ],
+        compiler_params=pltpu.CompilerParams(
+            collective_id=2, has_side_effects=True, vmem_limit_bytes=8 << 20
+        ),
+        name="gather_scores",
+    )(scores)
+
+
 def star_devices(feature_maps, coef_table, star_counts, star_cells, star_bands, psf_cotangent):
     groups = lax.axis_size("star")
     lanes = lax.axis_size("row")
@@ -429,7 +649,8 @@
 
     wavelength = 0.55 + 0.35 * band_ids.astype(F32) / (BANDS - 1)
     turns = phase_turns(mine(1.0 / wavelength), mine(coef_rows), feature_maps)
-    turns = lax.all_to_all(turns, "row", split_axis=0, concat_axis=0, tiled=True)
+    turns = row_exchange(turns, 0)
+    incoming, turns = lax.optimization_barrier((incoming, turns))
     cotangent = jnp.take(
         incoming, mine(owner) * capacity + mine(within) // groups, axis=0, mode="clip"
     )
@@ -440,27 +661,26 @@
     path_grad = star_gradient(
         my_wave, turns.reshape(size, size), cotangent.reshape(size, size), right, left
     )
-    path_grad = lax.all_to_all(
-        path_grad.reshape(lanes, row_count, size), "row", split_axis=0, concat_axis=0, tiled=True
-    )
-    path_grads = lax.all_gather(path_grad, "star", axis=0, tiled=True)
+    path_grads = gather_grads(path_grad.reshape(lanes, row_count, size), groups)
+    path_grads = path_grads.reshape(total, row_count, size)
     my_coefs = lax.dynamic_slice_in_dim(coef_rows.T, my_group * share, share, 0)
     map_grad, scores = map_sums(my_group, my_coefs, path_grads, feature_maps, share)
-    coef_part = lax.dot_general(
+    scores = jnp.pad(scores, ((0, 0), (0, -total % 128)))
+    scores = jnp.sum(gather_scores(scores, groups, lanes), axis=1)
+    scores = scores.reshape(map_count, -1)[:, :total]
+    coef_grad = lax.dot_general(
         cell_hot.astype(F32),
         scores * (1.0 / (8 * size)),
         (((0,), (1,)), ((), ())),
         precision=lax.Precision.HIGHEST,
     )
-    placed = lax.dynamic_update_slice_in_dim(
-        jnp.zeros((cell_count, map_count), F32), coef_part, my_group * share, 1
-    )
-    return map_grad, lax.psum(placed, ("star", "row"))
+    return map_grad, coef_grad
 
 
 def solution(mesh):
     placed = (P(None, "row", None), P(), P(), P(), P(), P("star", "row", None))
-    device = star_devices if mesh.shape["row"] == LIVE_DEV else per_device
+    fits = mesh.shape["row"] == LIVE_DEV and mesh.shape["star"] == PLANE_DEV
+    device = star_devices if fits else per_device
     return jax.shard_map(
         device,
         mesh=mesh,

time: 467 us -> 317 us (0.68)
  waiting for transfers between devices: 247 us -> 73.9 us
  Pallas kernels: 66.7 us -> 202 us
  blocking collectives: 92.3 us -> 0 us
  between operations: 14.2 us -> 0.78 us
    pallas_call x0 -> x3, Pallas kernels: none -> 137 us  [the longest x1 83.9 us: gather_grads(): pl.pallas_call(functools.partial(gather_kernel, lanes), out_shape=jax.Sha...]
    all_gather x1 -> x0, waiting for transfers between devices: 88.1 us -> none  [star_devices(): path_grads = lax.all_gather(path_grad, 'star', axis=0, tiled=True)]
    all_to_all x1 -> x0, blocking collectives: 52.2 us -> none  [star_devices(): lax.all_to_all(path_grad.reshape(lanes, row_count, size), 'row', split_ax...]
    all_to_all x1, waiting for transfers between devices: 72 us -> 31.4 us  [star_devices(): lax.all_to_all(outgoing, 'star', split_axis=0, concat_axis=0, tiled=True)]
    psum x1 -> x0, blocking collectives: 40.1 us -> none  [star_devices(): return (map_grad, lax.psum(placed, ('star', 'row')))]
    all_to_all x1 -> x0, waiting for transfers between devices: 39.7 us -> none  [star_devices(): lax.all_to_all(turns, 'row', split_axis=0, concat_axis=0, tiled=True)]
    all_to_all x1 -> x0, starting transfers between devices: 5.66 us -> none  [star_devices(): lax.all_to_all(turns, 'row', split_axis=0, concat_axis=0, tiled=True)]
  transfers between devices with their start and end apart: 4 -> 2, of which waited for: 4 -> 2; matrix products, arithmetic and copies ran while one was open for 2% -> 2% of each run, Pallas kernels for 4% -> 19%
where the time goes in v2:
time: 317 us; the launch traced here: 316 us
  Pallas kernels  202 us (64%)
  waiting for transfers between devices  73.9 us (23%)
  local copies, waits for them, and re-layouts  22.7 us (7%)
  starting transfers between devices  11 us (3%)
  other arithmetic  3.96 us (1%)
    pallas_call x1, Pallas kernels, gather_grads(): pl.pallas_call(functools.partial(gather_kernel, lanes), out_shape=jax.Sha...  83.9 us
    all_to_all x1, waiting for transfers between devices, star_devices(): lax.all_to_all(cotangent, 'row', split_axis=0, concat_axis=0, tiled=True)  42.6 us
    pallas_call x1, Pallas kernels, row_exchange(): pl.pallas_call(functools.partial(row_kernel, lanes), out_shape=jax.ShapeD...  40.1 us
    all_to_all x1, waiting for transfers between devices, star_devices(): lax.all_to_all(outgoing, 'star', split_axis=0, concat_axis=0, tiled=True)  31.4 us
    pallas_call x1, Pallas kernels, star_gradient(): pl.pallas_call(functools.partial(star_kernel, 128), out_shape=jax.ShapeDt...  29.8 us
    pallas_call x1, Pallas kernels, phase_turns(): pl.pallas_call(phase_kernel, out_shape=jax.ShapeDtypeStruct((stars, row_c...  18.7 us
    pallas_call x1, Pallas kernels, map_sums(): pl.pallas_call(maps_kernel, out_shape=(jax.ShapeDtypeStruct((share, row_c...  17.3 us
    pallas_call x1, Pallas kernels, gather_scores(): pl.pallas_call(functools.partial(score_kernel, groups, lanes), out_shape=...  12.6 us
  transfers between devices with their start and end apart: 2, of which 2 were waited for; matrix products, arithmetic and copies ran while one was open for 2% of the time, Pallas kernels for 19%

profile of v2, /device:TPU:0, one launch (start us, length us, event | category | flops | bytes accessed | tf_op | source)
XLA Modules:
  0.0 315.9 jit_solution(1105440382506970181)
XLA Ops:
  0.6 0.0 copy-start
  0.7 0.8 reduce-window.8
  1.5 1.3 fusion.10
  2.8 0.7 and_select_fusion.1
  3.4 0.1 add_minimum_fusion
  3.5 0.1 reshape.168
  3.6 7.7 %gather_fusion = bf16[16,256,1024]{2,1,0:T(8,128)(2,1)} fusion(bf16[12,256,1024]{2,1,0:T(8,128)(2,1)} %param.13, s32[1024]{0:T(1024)S(1)} %pad_clamp_fusion.1), kind=kCustom, calls=%fused_computation | custom fusion | bytes 16777280 | tf_op jit(solution)/shard_map/jit(_take)/gather | solution.py:629
  11.3 0.0 copy-start.5
  11.3 0.0 copy-start.6
  11.3 5.3 %all-to-all-start = ((bf16[16,256,1024]{2,1,0:T(8,128)(2,1)}), bf16[16,256,1024]{2,1,0:T(8,128)(2,1)}, u32[]{:S(2)}, u32[]{:S(2)}) async-start(bf16[16,256,1024]{2,1,0:T(8,128)(2,1)} %gather_fusion), calls=%async_computation | async-start | bytes 16777216 | tf_op jit(solution)/shard_map/all_to_all | solution.py:632
  16.6 0.0 copy-done.5
  16.6 0.1 broadcast_in_dim.70
  16.7 0.0 copy-done.6
  16.7 0.1 broadcast_in_dim.73
  16.8 0.1 convert_reduce_fusion
  16.9 0.1 select_reduce_fusion.2
  17.0 0.2 select_reduce_fusion
  17.2 0.0 copy-done
  17.2 0.2 convolution_convert_fusion
  17.4 0.1 broadcast_multiply_fusion
  17.5 1.8 mul.110.weight_ref
  19.3 0.1 dynamic_slice.20.inverse_ref
  19.4 18.7 %phase_turns.1.in_ref = bf16[4,256,1024]{2,1,0:T(8,128)(2,1)S(1)} custom-call(f32[4]{0:T(128)S(1)} %dynamic_slice.20.inverse_ref, bf16[64,1024]{1,0:T(8,128)(2,1)S(1)} %mul.110.weight_ref, bf16[64,256,1024]{2,1,0:T(8,128)(2,1)} %maps_ref.3), custom_call_target="tpu_custom_call" | custom-call | flops 2147483648 | bytes 35651584 | tf_op jit(solution)/shard_map/phase_turns/pallas_call | solution.py:205
  38.1 40.1 %row_exchange.1 = bf16[4,256,1024]{2,1,0:T(8,128)(2,1)S(1)} custom-call(bf16[4,256,1024]{2,1,0:T(8,128)(2,1)S(1)} %phase_turns.1.in_ref), custom_call_target="tpu_custom_call" | custom-call | bytes 104857600 | tf_op jit(solution)/shard_map/row_exchange/pallas_call | solution.py:439
  78.3 0.0 copy-start.3
  78.3 1.4 copy-done.3
  79.7 0.1 fusion.12
  79.8 31.4 %all-to-all-done = bf16[16,256,1024]{2,1,0:T(8,128)(2,1)} async-done(((bf16[16,256,1024]{2,1,0:T(8,128)(2,1)}), bf16[16,256,1024]{2,1,0:T(8,128)(2,1)}, u32[]{:S(2)}, u32[]{:S(2)}) %all-to-all-start) | async-done | bytes 8388640 | tf_op jit(solution)/shard_map/all_to_all | solution.py:632
  111.1 5.4 %gather_fusion.1 = bf16[4,256,1024]{2,1,0:T(8,128)(2,1)} fusion(bf16[16,256,1024]{2,1,0:T(8,128)(2,1)} %all-to-all-done, s32[1024]{0:T(1024)S(1)} %pad_clamp_fusion), kind=kCustom, calls=%fused_computation.1 | custom fusion | bytes 4194320 | tf_op jit(solution)/shard_map/jit(_take)/gather | solution.py:654
  116.5 5.7 %all-to-all-start.1 = ((bf16[4,256,1024]{2,1,0:T(8,128)(2,1)}), bf16[4,256,1024]{2,1,0:T(8,128)(2,1)S(1)}, u32[]{:S(2)}, u32[]{:S(2)}) async-start(bf16[4,256,1024]{2,1,0:T(8,128)(2,1)} %gather_fusion.1), calls=%async_computation.1 | async-start | bytes 4194304 | tf_op jit(solution)/shard_map/all_to_all | solution.py:657
  122.2 0.1 dynamic-slice_bitcast_fusion
  122.2 0.1 copy.12
  122.3 0.1 broadcast_multiply_fusion.1
  122.5 1.8 mul.104.weight_ref
  124.3 0.6 dynamic_slice.19.wave_ref
  124.9 42.6 %all-to-all-done.1 = bf16[4,256,1024]{2,1,0:T(8,128)(2,1)S(1)} async-done(((bf16[4,256,1024]{2,1,0:T(8,128)(2,1)}), bf16[4,256,1024]{2,1,0:T(8,128)(2,1)S(1)}, u32[]{:S(2)}, u32[]{:S(2)}) %all-to-all-start.1) | async-done | bytes 2097184 | tf_op jit(solution)/shard_map/all_to_all | solution.py:657
  167.4 0.0 copy-start.4
  167.4 1.3 copy-done.4
  168.7 29.8 %star_gradient.1 = bf16[1024,1024]{1,0:T(8,128)(2,1)} custom-call(f32[1]{0:T(128)} %dynamic_slice.19.wave_ref, bf16[1024,1024]{1,0:T(8,128)(2,1)} %bitcast.19, bf16[1024,1024]{1,0:T(8,128)(2,1)} %bitcast.20, bf16[4,512,512]{2,1,0:T(8,128)(2,1)} %constant.106.clone.right_ref, bf16[4,512,512]{2,1,0:T(8,128)(2,1)} %constant.107.clone.left_ref), custom_call_target="tpu_custom_call" | custom-call | tf_op jit(solution)/shard_map/star_gradient/pallas_call | solution.py:327
  198.5 0.0 copy-start.2
  198.5 1.6 copy-done.2
  200.1 83.9 %gather_grads.1 = bf16[8,4,256,1024]{3,2,1,0:T(8,128)(2,1)S(1)} custom-call(bf16[4,256,1024]{2,1,0:T(8,128)(2,1)S(1)} %bitcast.18), custom_call_target="tpu_custom_call" | custom-call | tf_op jit(solution)/shard_map/gather_grads/pallas_call | solution.py:545
  284.0 17.3 %map_sums.1 = (f32[8,256,1024]{2,1,0:T(8,128)}, f32[128,512]{1,0:T(8,128)S(1)}) custom-call(s32[1]{0:T(128)} %bitcast.group_ref, bf16[128,512]{1,0:T(8,128)(2,1)S(1)} %mul.104.weight_ref, bf16[32,256,1024]{2,1,0:T(8,128)(2,1)S(1)} %bitcast.17, bf16[64,256,1024]{2,1,0:T(8,128)(2,1)} %maps_ref.3), custom_call_target="tpu_custom_call" | custom-call | tf_op jit(solution)/shard_map/map_sums/pallas_call | solution.py:366
  301.3 0.7 reshape.164
  302.0 0.3 multiply_reduce_fusion
  302.4 12.6 %gather_scores.1 = f32[8,4,8,128]{3,2,1,0:T(8,128)S(1)} custom-call(f32[8,128]{1,0:T(8,128)S(1)} %pad.4.in_ref), custom_call_target="tpu_custom_call" | custom-call | tf_op jit(solution)/shard_map/gather_scores/pallas_call | solution.py:594
  315.0 0.9 fusion
  315.9 0.0 copy-done.1
  (12 shorter events, 0.1 us)
Async XLA Ops:
  0.6 16.5 %copy-start = (bf16[64,64]{1,0:T(8,128)(2,1)S(1)}, bf16[64,64]{1,0:T(8,128)(2,1)}, u32[]{:S(2)}) copy-start(bf16[64,64]{1,0:T(8,128)(2,1)} %param.9) | copy-start | bytes 24580
  11.3 5.3 %copy-start.5 = (s32[8,12]{1,0:T(8,128)S(1)}, s32[8,12]{1,0:T(8,128)}, u32[]{:S(2)}) copy-start(s32[8,12]{1,0:T(8,128)} %param.11) | copy-start | bytes 1156
  11.3 5.4 %copy-start.6 = (s32[8,12]{1,0:T(8,128)S(1)}, s32[8,12]{1,0:T(8,128)}, u32[]{:S(2)}) copy-start(s32[8,12]{1,0:T(8,128)} %param.12) | copy-start | bytes 1156
  11.3 99.8 %all-to-all-start = ((bf16[16,256,1024]{2,1,0:T(8,128)(2,1)}), bf16[16,256,1024]{2,1,0:T(8,128)(2,1)}, u32[]{:S(2)}, u32[]{:S(2)}) async-start(bf16[16,256,1024]{2,1,0:T(8,128)(2,1)} %gather_fusion), calls=%async_computation | async-start | bytes 16777216 | tf_op jit(solution)/shard_map/all_to_all | solution.py:632
  78.3 1.4 copy-start.3
  116.5 50.9 %all-to-all-start.1 = ((bf16[4,256,1024]{2,1,0:T(8,128)(2,1)}), bf16[4,256,1024]{2,1,0:T(8,128)(2,1)S(1)}, u32[]{:S(2)}, u32[]{:S(2)}) async-start(bf16[4,256,1024]{2,1,0:T(8,128)(2,1)} %gather_fusion.1), calls=%async_computation.1 | async-start | bytes 4194304 | tf_op jit(solution)/shard_map/all_to_all | solution.py:657
  167.4 1.3 copy-start.4
  198.5 1.6 copy-start.2
  301.3 14.5 %copy-start.1 = (bf16[64,64]{1,0:T(8,128)(2,1)S(1)}, bf16[64,64]{1,0:T(8,128)(2,1)}, u32[]{:S(2)}) copy-start(bf16[64,64]{1,0:T(8,128)(2,1)} %param.9) | copy-start | bytes 24580

commit v3 on v2

--- a/solution.py
+++ b/solution.py
@@ -411,49 +411,110 @@
     )
 
 
-def row_kernel(lanes, in_ref, out_ref, local_sem, send_sem, recv_sem):
+DELIVER_STEPS = 4
+
+
+def deliver_kernel(
+    groups, lanes, pick_ref, turns_ref, cot_ref, turns_out, cot_out, stage, *scratch
+):
+    arrived, sems = scratch[:DELIVER_STEPS], scratch[DELIVER_STEPS:]
+    t_local, t_send, t_recv, s_local, s_send, s_recv, z_local, z_send, z_recv = sems
     row = lax.axis_index("row")
-    peers = [{"row": (row + d) % lanes} for d in range(1, lanes)]
-    greet(peers)
-    copies = [
+    me = lax.axis_index("star")
+    capacity = cot_ref.shape[1]
+    depth = cot_ref.shape[2] // DELIVER_STEPS
+    row_peers = [{"row": (row + d) % lanes} for d in range(1, lanes)]
+    star_peers = [{"star": (me + d) % groups} for d in range(1, groups)]
+    greet(row_peers + star_peers)
+    turns = [
         send(
-            in_ref.at[(row + d) % lanes],
-            out_ref.at[row],
-            send_sem.at[d - 1],
-            recv_sem.at[d - 1],
-            peers[d - 1],
+            turns_ref.at[(row + d) % lanes],
+            turns_out.at[row],
+            t_send.at[d - 1],
+            t_recv.at[d - 1],
+            row_peers[d - 1],
         )
         for d in range(1, lanes)
     ]
-    for copy in copies:
+    turns.append(pltpu.make_async_copy(turns_ref.at[row], turns_out.at[row], t_local))
+    for copy in turns:
         copy.start()
-    own = pltpu.make_async_copy(in_ref.at[row], out_ref.at[row], local_sem)
-    own.start()
-    own.wait()
-    for copy in copies:
+    steps = []
+    for step in range(DELIVER_STEPS):
+        rows = pl.ds(step * depth, depth)
+        target = arrived[step].at[pl.ds(me * capacity, capacity)]
+        copies = [
+            send(
+                cot_ref.at[(me + d) % groups, :, rows],
+                target,
+                s_send.at[step, d - 1],
+                s_recv.at[step, d - 1],
+                star_peers[d - 1],
+            )
+            for d in range(1, groups)
+        ]
+        copies.append(pltpu.make_async_copy(cot_ref.at[me, :, rows], target, s_local.at[step]))
+        for copy in copies:
+            copy.start()
+        steps.append(copies)
+    sent = []
+    for step in range(DELIVER_STEPS):
+        rows = pl.ds(step * depth, depth)
+        for copy in steps[step]:
+            copy.wait()
+        for lane in range(lanes):
+            stage[lane, rows] = arrived[step][pick_ref[lane]]
+        copies = [
+            send(
+                stage.at[(row + d) % lanes, rows],
+                cot_out.at[row, rows],
+                z_send.at[step, d - 1],
+                z_recv.at[step, d - 1],
+                row_peers[d - 1],
+            )
+            for d in range(1, lanes)
+        ]
+        copies.append(
+            pltpu.make_async_copy(stage.at[row, rows], cot_out.at[row, rows], z_local.at[step])
+        )
+        for copy in copies:
+            copy.start()
+        sent += copies
+    for copy in turns + sent:
         copy.wait()
 
 
-def row_exchange(blocks, collective_id):
-    lanes = blocks.shape[0]
+def deliver(picks, turns, outgoing):
+    groups, capacity, row_count, size = outgoing.shape
+    lanes = turns.shape[0]
+    depth = row_count // DELIVER_STEPS
+    dma = pltpu.SemaphoreType.DMA
+    hbm = pl.BlockSpec(memory_space=pl.ANY)
+    vmem = pl.BlockSpec(memory_space=pltpu.VMEM)
+    shape = jax.ShapeDtypeStruct((lanes, row_count, size), BF16)
     return pl.pallas_call(
-        functools.partial(row_kernel, lanes),
-        out_shape=jax.ShapeDtypeStruct(blocks.shape, blocks.dtype),
-        in_specs=[pl.BlockSpec(memory_space=pltpu.VMEM)],
-        out_specs=pl.BlockSpec(memory_space=pl.ANY),
-        scratch_shapes=[
-            pltpu.SemaphoreType.DMA,
-            pltpu.SemaphoreType.DMA((lanes - 1,)),
-            pltpu.SemaphoreType.DMA((lanes - 1,)),
+        functools.partial(deliver_kernel, groups, lanes),
+        out_shape=(shape, shape),
+        in_specs=[pl.BlockSpec(memory_space=pltpu.SMEM), vmem, hbm],
+        out_specs=(hbm, hbm),
+        scratch_shapes=[pltpu.VMEM((lanes, row_count, size), BF16)]
+        + [pltpu.VMEM((groups * capacity, depth, size), BF16)] * DELIVER_STEPS
+        + [
+            dma,
+            dma((lanes - 1,)),
+            dma((lanes - 1,)),
+            dma((DELIVER_STEPS,)),
+            dma((DELIVER_STEPS, groups - 1)),
+            dma((DELIVER_STEPS, groups - 1)),
+            dma((DELIVER_STEPS,)),
+            dma((DELIVER_STEPS, lanes - 1)),
+            dma((DELIVER_STEPS, lanes - 1)),
         ],
         compiler_params=pltpu.CompilerParams(
-            collective_id=collective_id, has_side_effects=True, vmem_limit_bytes=8 << 20
+            collective_id=0, has_side_effects=True, vmem_limit_bytes=20 << 20
         ),
-        cost_estimate=pl.CostEstimate(
-            flops=0, bytes_accessed=50 * blocks.size * 2, transcendentals=0
-        ),
-        name="row_exchange",
-    )(blocks)
+        name="deliver",
+    )(picks, turns, outgoing)
 
 
 def gather_kernel(lanes, in_ref, out_ref, local, z_send, z_recv, p_send, p_recv, c_send, c_recv):
@@ -629,7 +690,7 @@
     outgoing = jnp.take(
         psf_cotangent, jnp.minimum(send_slot, slot_count - 1), axis=0, mode="clip"
     )
-    incoming = lax.all_to_all(outgoing, "star", split_axis=0, concat_axis=0, tiled=True)
+    outgoing = outgoing.reshape((groups, capacity) + outgoing.shape[1:])
 
     total = groups * lanes
     order = jnp.arange(total, dtype=jnp.int32)
@@ -649,12 +710,8 @@
 
     wavelength = 0.55 + 0.35 * band_ids.astype(F32) / (BANDS - 1)
     turns = phase_turns(mine(1.0 / wavelength), mine(coef_rows), feature_maps)
-    turns = row_exchange(turns, 0)
-    incoming, turns = lax.optimization_barrier((incoming, turns))
-    cotangent = jnp.take(
-        incoming, mine(owner) * capacity + mine(within) // groups, axis=0, mode="clip"
-    )
-    cotangent = lax.all_to_all(cotangent, "row", split_axis=0, concat_axis=0, tiled=True)
+    picks = mine(owner) * capacity + mine(within) // groups
+    turns, cotangent = deliver(picks, turns, outgoing)
     wave = wave_numbers(band_ids)
     my_wave = lax.dynamic_slice_in_dim(wave, my_group * lanes + my_lane, 1, 0)
     right, left = quarter_tables(size)

time: 317 us -> 312 us (0.984)
  waiting for transfers between devices: 73.9 us -> 0 us
  Pallas kernels: 202 us -> 271 us
  starting transfers between devices: 11 us -> 0 us
  local copies, waits for them, and re-layouts: 22.7 us -> 33.5 us
    all_to_all x2 -> x0, waiting for transfers between devices: 73.9 us -> none  [the longest x1 42.6 us: star_devices(): lax.all_to_all(cotangent, 'row', split_axis=0, concat_axis=0, tiled=True)]
    pallas_call x1, Pallas kernels: 40.1 us -> 108 us  [deliver(): pl.pallas_call(functools.partial(deliver_kernel, groups, lanes), out_shap...]
    unnamed x14 -> x16, local copies, waits for them, and re-layouts: 4.32 us -> 19.1 us
    all_to_all x2 -> x0, starting transfers between devices: 11 us -> none  [the longest x1 5.66 us: star_devices(): lax.all_to_all(cotangent, 'row', split_axis=0, concat_axis=0, tiled=True)]
    gather x1 -> x0, local copies, waits for them, and re-layouts: 5.38 us -> none  [star_devices(): jnp.take(incoming, mine(owner) * capacity + mine(within) // groups, axis=...]
  transfers between devices with their start and end apart: 2 -> 0, of which waited for: 2 -> 0; matrix products, arithmetic and copies ran while one was open for 2% -> 0% of each run, Pallas kernels for 19% -> 0%
where the time goes in v3:
time: 312 us; the launch traced here: 311 us
  Pallas kernels  271 us (87%)
  local copies, waits for them, and re-layouts  33.5 us (11%)
  other arithmetic  3.96 us (1%)
    pallas_call x1, Pallas kernels, deliver(): pl.pallas_call(functools.partial(deliver_kernel, groups, lanes), out_shap...  108 us
    pallas_call x1, Pallas kernels, gather_grads(): pl.pallas_call(functools.partial(gather_kernel, lanes), out_shape=jax.Sha...  86.1 us
    pallas_call x1, Pallas kernels, star_gradient(): pl.pallas_call(functools.partial(star_kernel, 128), out_shape=jax.ShapeDt...  29.7 us
    unnamed x16, local copies, waits for them, and re-layouts  19.1 us
    pallas_call x1, Pallas kernels, phase_turns(): pl.pallas_call(phase_kernel, out_shape=jax.ShapeDtypeStruct((stars, row_c...  18.7 us
    pallas_call x1, Pallas kernels, map_sums(): pl.pallas_call(maps_kernel, out_shape=(jax.ShapeDtypeStruct((share, row_c...  17.2 us
    pallas_call x1, Pallas kernels, gather_scores(): pl.pallas_call(functools.partial(score_kernel, groups, lanes), out_shape=...  11.3 us
    gather x1, local copies, waits for them, and re-layouts, star_devices(): jnp.take(psf_cotangent, jnp.minimum(send_slot, slot_count - 1), axis=0, m...  7.69 us

profile of v3, /device:TPU:0, one launch (start us, length us, event | category | flops | bytes accessed | tf_op | source)
XLA Modules:
  0.0 310.8 jit_solution(2894405073379313689)
XLA Ops:
  0.6 0.0 copy-start
  0.7 0.8 reduce-window.8
  1.5 1.3 fusion.10
  2.8 0.1 convert_reduce_fusion
  2.9 0.1 select_reduce_fusion.2
  3.0 0.8 broadcast_in_dim.66
  3.7 0.8 broadcast_in_dim.69
  4.5 0.2 select_reduce_fusion
  4.7 0.0 copy-done
  4.7 0.2 convolution_convert_fusion
  4.9 0.1 broadcast_multiply_fusion
  5.1 1.8 mul.110.weight_ref
  6.8 0.1 dynamic_slice.22.inverse_ref
  6.9 18.7 %phase_turns.1.turns_ref = bf16[4,256,1024]{2,1,0:T(8,128)(2,1)S(1)} custom-call(f32[4]{0:T(128)S(1)} %dynamic_slice.22.inverse_ref, bf16[64,1024]{1,0:T(8,128)(2,1)S(1)} %mul.110.weight_ref, bf16[64,256,1024]{2,1,0:T(8,128)(2,1)} %maps_ref.3), custom_call_target="tpu_custom_call" | custom-call | flops 2147483648 | bytes 35651584 | tf_op jit(solution)/shard_map/phase_turns/pallas_call | solution.py:205
  25.6 0.1 fusion.12.pick_ref
  25.7 0.7 and_select_fusion
  26.4 0.1 add_minimum_fusion
  26.5 0.1 reshape.172
  26.6 7.7 %gather_fusion = bf16[16,256,1024]{2,1,0:T(8,128)(2,1)} fusion(bf16[12,256,1024]{2,1,0:T(8,128)(2,1)} %param.13, s32[1024]{0:T(1024)S(1)} %pad_clamp_fusion), kind=kCustom, calls=%fused_computation | custom fusion | bytes 16777280 | tf_op jit(solution)/shard_map/jit(_take)/gather | solution.py:690
  34.2 0.0 copy-start.4
  34.2 3.4 %copy-done.4 = bf16[16,256,1024]{2,1,0:T(8,128)(2,1)S(1)} copy-done((bf16[16,256,1024]{2,1,0:T(8,128)(2,1)S(1)}, bf16[16,256,1024]{2,1,0:T(8,128)(2,1)}, u32[]{:S(2)}) %copy-start.4) | copy-done | bytes 8388632
  37.6 108.4 %deliver.1 = (bf16[4,256,1024]{2,1,0:T(8,128)(2,1)S(1)}, bf16[4,256,1024]{2,1,0:T(8,128)(2,1)S(1)}) custom-call(s32[4]{0:T(128)S(1)} %fusion.12.pick_ref, bf16[4,256,1024]{2,1,0:T(8,128)(2,1)S(1)} %phase_turns.1.turns_ref, bf16[8,2,256,1024]{3,2,1,0:T(8,128)(2,1)S(1)} %bitcast.19), custom_call_target="tpu_custom_call" | custom-call | tf_op jit(solution)/shard_map/deliver/pallas_call | solution.py:495
  146.0 0.0 copy-start.6
  146.0 1.3 copy-done.6
  147.4 0.0 copy-start.7
  147.4 1.3 copy-done.7
  148.7 0.6 dynamic_slice.19.wave_ref
  149.3 29.7 %star_gradient.1 = bf16[1024,1024]{1,0:T(8,128)(2,1)} custom-call(f32[1]{0:T(128)} %dynamic_slice.19.wave_ref, bf16[1024,1024]{1,0:T(8,128)(2,1)} %bitcast.21, bf16[1024,1024]{1,0:T(8,128)(2,1)} %bitcast.22, bf16[4,512,512]{2,1,0:T(8,128)(2,1)} %constant.106.clone.right_ref, bf16[4,512,512]{2,1,0:T(8,128)(2,1)} %constant.107.clone.left_ref), custom_call_target="tpu_custom_call" | custom-call | tf_op jit(solution)/shard_map/star_gradient/pallas_call | solution.py:327
  179.0 0.0 copy-start.5
  179.0 1.6 copy-done.5
  180.6 86.1 %gather_grads.1 = bf16[8,4,256,1024]{3,2,1,0:T(8,128)(2,1)S(1)} custom-call(bf16[4,256,1024]{2,1,0:T(8,128)(2,1)S(1)} %bitcast.20), custom_call_target="tpu_custom_call" | custom-call | tf_op jit(solution)/shard_map/gather_grads/pallas_call | solution.py:606
  266.7 0.0 copy-start.2
  266.7 5.7 %copy-done.2 = bf16[8,4,256,1024]{3,2,1,0:T(8,128)(2,1)} copy-done((bf16[8,4,256,1024]{3,2,1,0:T(8,128)(2,1)}, bf16[8,4,256,1024]{3,2,1,0:T(8,128)(2,1)S(1)}, u32[]{:S(2)}) %copy-start.2) | copy-done | bytes 16777240
  272.4 0.1 dynamic-slice_bitcast_fusion
  272.5 0.1 copy.12
  272.6 0.1 broadcast_multiply_fusion.1
  272.7 1.8 mul.104.weight_ref
  274.5 0.0 copy-start.3
  274.5 5.8 %copy-done.3 = bf16[8,4,256,1024]{3,2,1,0:T(8,128)(2,1)S(1)} copy-done((bf16[8,4,256,1024]{3,2,1,0:T(8,128)(2,1)S(1)}, bf16[8,4,256,1024]{3,2,1,0:T(8,128)(2,1)}, u32[]{:S(2)}) %copy-start.3) | copy-done | bytes 16777240
  280.3 17.2 %map_sums.1 = (f32[8,256,1024]{2,1,0:T(8,128)}, f32[128,512]{1,0:T(8,128)S(1)}) custom-call(s32[1]{0:T(128)} %bitcast.group_ref, bf16[128,512]{1,0:T(8,128)(2,1)S(1)} %mul.104.weight_ref, bf16[32,256,1024]{2,1,0:T(8,128)(2,1)S(1)} %bitcast.18, bf16[64,256,1024]{2,1,0:T(8,128)(2,1)} %maps_ref.3), custom_call_target="tpu_custom_call" | custom-call | tf_op jit(solution)/shard_map/map_sums/pallas_call | solution.py:366
  297.5 0.0 copy-start.1
  297.5 0.7 reshape.168
  298.2 0.3 multiply_reduce_fusion
  298.6 11.3 %gather_scores.1 = f32[8,4,8,128]{3,2,1,0:T(8,128)S(1)} custom-call(f32[8,128]{1,0:T(8,128)S(1)} %pad.4.in_ref), custom_call_target="tpu_custom_call" | custom-call | tf_op jit(solution)/shard_map/gather_scores/pallas_call | solution.py:655
  309.9 0.9 fusion
  310.8 0.0 copy-done.1
  (10 shorter events, 0.1 us)
Async XLA Ops:
  0.6 4.1 %copy-start = (bf16[64,64]{1,0:T(8,128)(2,1)S(1)}, bf16[64,64]{1,0:T(8,128)(2,1)}, u32[]{:S(2)}) copy-start(bf16[64,64]{1,0:T(8,128)(2,1)} %param.9) | copy-start | bytes 24580
  34.2 3.4 %copy-start.4 = (bf16[16,256,1024]{2,1,0:T(8,128)(2,1)S(1)}, bf16[16,256,1024]{2,1,0:T(8,128)(2,1)}, u32[]{:S(2)}) copy-start(bf16[16,256,1024]{2,1,0:T(8,128)(2,1)} %gather_fusion) | copy-start | bytes 25165828
  146.0 1.3 copy-start.6
  147.4 1.4 copy-start.7
  179.0 1.6 copy-start.5
  266.7 5.7 %copy-start.2 = (bf16[8,4,256,1024]{3,2,1,0:T(8,128)(2,1)}, bf16[8,4,256,1024]{3,2,1,0:T(8,128)(2,1)S(1)}, u32[]{:S(2)}) copy-start(bf16[8,4,256,1024]{3,2,1,0:T(8,128)(2,1)S(1)} %gather_grads.1) | copy-start | bytes 50331652
  274.5 5.8 %copy-start.3 = (bf16[8,4,256,1024]{3,2,1,0:T(8,128)(2,1)S(1)}, bf16[8,4,256,1024]{3,2,1,0:T(8,128)(2,1)}, u32[]{:S(2)}) copy-start(bf16[8,4,256,1024]{3,2,1,0:T(8,128)(2,1)} %copy-done.2) | copy-start | bytes 50331652
  297.5 13.2 %copy-start.1 = (bf16[64,64]{1,0:T(8,128)(2,1)S(1)}, bf16[64,64]{1,0:T(8,128)(2,1)}, u32[]{:S(2)}) copy-start(bf16[64,64]{1,0:T(8,128)(2,1)} %param.9) | copy-start | bytes 24580

commit v4 on v3

--- a/solution.py
+++ b/solution.py
@@ -382,7 +382,7 @@
                 pl.BlockSpec(score_shape, lambda i, g: (0, 0)),
             ),
         ),
-        compiler_params=pltpu.CompilerParams(vmem_limit_bytes=24 << 20),
+        compiler_params=pltpu.CompilerParams(vmem_limit_bytes=56 << 20),
         name="map_sums",
     )(my_group[None], weights, path_grads, feature_maps)
     eye = jnp.eye(ROWS_STEP, dtype=F32)
@@ -511,7 +511,7 @@
             dma((DELIVER_STEPS, lanes - 1)),
         ],
         compiler_params=pltpu.CompilerParams(
-            collective_id=0, has_side_effects=True, vmem_limit_bytes=20 << 20
+            collective_id=0, has_side_effects=True, vmem_limit_bytes=56 << 20
         ),
         name="deliver",
     )(picks, turns, outgoing)
@@ -618,7 +618,7 @@
             dma((GATHER_STEPS, 4)),
         ],
         compiler_params=pltpu.CompilerParams(
-            collective_id=1, has_side_effects=True, vmem_limit_bytes=8 << 20
+            collective_id=1, has_side_effects=True, vmem_limit_bytes=56 << 20
         ),
         name="gather_grads",
     )(path_grad)

time: 312 us -> 303 us (0.971)
  local copies, waits for them, and re-layouts: 33.5 us -> 17.5 us
  Pallas kernels: 271 us -> 279 us
    unnamed x16 -> x6, local copies, waits for them, and re-layouts: 19.1 us -> 1.34 us
    pallas_call x1, Pallas kernels: 17.2 us -> 20.4 us  [map_sums(): pl.pallas_call(maps_kernel, out_shape=(jax.ShapeDtypeStruct((share, row_c...]
where the time goes in v4:
time: 303 us; the launch traced here: 302 us
  Pallas kernels  279 us (92%)
  local copies, waits for them, and re-layouts  17.5 us (6%)
  other arithmetic  4.47 us (1%)
    pallas_call x1, Pallas kernels, deliver(): pl.pallas_call(functools.partial(deliver_kernel, groups, lanes), out_shap...  110 us
    pallas_call x1, Pallas kernels, gather_grads(): pl.pallas_call(functools.partial(gather_kernel, lanes), out_shape=jax.Sha...  89 us
    pallas_call x1, Pallas kernels, star_gradient(): pl.pallas_call(functools.partial(star_kernel, 128), out_shape=jax.ShapeDt...  29.9 us
    pallas_call x1, Pallas kernels, map_sums(): pl.pallas_call(maps_kernel, out_shape=(jax.ShapeDtypeStruct((share, row_c...  20.4 us
    pallas_call x1, Pallas kernels, phase_turns(): pl.pallas_call(phase_kernel, out_shape=jax.ShapeDtypeStruct((stars, row_c...  18.7 us
    pallas_call x1, Pallas kernels, gather_scores(): pl.pallas_call(functools.partial(score_kernel, groups, lanes), out_shape=...  10.6 us
    gather x1, local copies, waits for them, and re-layouts, star_devices(): jnp.take(psf_cotangent, jnp.minimum(send_slot, slot_count - 1), axis=0, m...  7.69 us

profile of v4, /device:TPU:0, one launch (start us, length us, event | category | flops | bytes accessed | tf_op | source)
XLA Modules:
  0.0 302.3 jit_solution(1404273143138238085)
XLA Ops:
  0.6 0.0 copy-start
  0.7 0.8 reduce-window.8
  1.5 1.3 fusion.10
  2.8 0.1 convert_reduce_fusion
  2.9 0.1 select_reduce_fusion.2
  3.0 0.8 broadcast_in_dim.66
  3.7 0.8 broadcast_in_dim.69
  4.5 0.2 select_reduce_fusion
  4.7 0.0 copy-done
  4.7 0.2 convolution_convert_fusion
  4.9 0.1 broadcast_multiply_fusion
  5.1 1.8 mul.110.weight_ref
  6.8 0.1 dynamic_slice.22.inverse_ref
  6.9 18.7 %phase_turns.1.turns_ref = bf16[4,256,1024]{2,1,0:T(8,128)(2,1)S(1)} custom-call(f32[4]{0:T(128)S(1)} %dynamic_slice.22.inverse_ref, bf16[64,1024]{1,0:T(8,128)(2,1)S(1)} %mul.110.weight_ref, bf16[64,256,1024]{2,1,0:T(8,128)(2,1)} %maps_ref.3), custom_call_target="tpu_custom_call" | custom-call | flops 2147483648 | bytes 35651584 | tf_op jit(solution)/shard_map/phase_turns/pallas_call | solution.py:205
  25.6 0.0 copy-start.2
  25.6 1.3 copy-done.2
  27.0 0.6 fusion.12.pick_ref
  27.6 0.7 and_select_fusion
  28.2 0.1 add_minimum_fusion
  28.3 0.1 reshape.172
  28.4 7.7 %gather_fusion = bf16[16,256,1024]{2,1,0:T(8,128)(2,1)} fusion(bf16[12,256,1024]{2,1,0:T(8,128)(2,1)} %param.13, s32[1024]{0:T(1024)S(1)} %pad_clamp_fusion), kind=kCustom, calls=%fused_computation | custom fusion | bytes 16777280 | tf_op jit(solution)/shard_map/jit(_take)/gather | solution.py:690
  36.1 109.9 %deliver.1 = (bf16[4,256,1024]{2,1,0:T(8,128)(2,1)}, bf16[4,256,1024]{2,1,0:T(8,128)(2,1)}) custom-call(s32[4]{0:T(128)} %fusion.12.pick_ref, bf16[4,256,1024]{2,1,0:T(8,128)(2,1)} %copy-done.2, bf16[8,2,256,1024]{3,2,1,0:T(8,128)(2,1)} %bitcast.19), custom_call_target="tpu_custom_call" | custom-call | tf_op jit(solution)/shard_map/deliver/pallas_call | solution.py:495
  146.0 0.6 dynamic_slice.19.wave_ref
  146.6 29.9 %star_gradient.1 = bf16[1024,1024]{1,0:T(8,128)(2,1)} custom-call(f32[1]{0:T(128)} %dynamic_slice.19.wave_ref, bf16[1024,1024]{1,0:T(8,128)(2,1)} %bitcast.21, bf16[1024,1024]{1,0:T(8,128)(2,1)} %bitcast.22, bf16[4,512,512]{2,1,0:T(8,128)(2,1)} %constant.106.clone.right_ref, bf16[4,512,512]{2,1,0:T(8,128)(2,1)} %constant.107.clone.left_ref), custom_call_target="tpu_custom_call" | custom-call | tf_op jit(solution)/shard_map/star_gradient/pallas_call | solution.py:327
  176.6 89.0 %gather_grads.1 = bf16[8,4,256,1024]{3,2,1,0:T(8,128)(2,1)} custom-call(bf16[4,256,1024]{2,1,0:T(8,128)(2,1)} %bitcast.20), custom_call_target="tpu_custom_call" | custom-call | tf_op jit(solution)/shard_map/gather_grads/pallas_call | solution.py:606
  265.5 0.1 dynamic-slice_bitcast_fusion
  265.6 0.1 copy.12
  265.7 0.1 broadcast_multiply_fusion.1
  265.9 2.5 mul.104.weight_ref
  268.3 20.4 %map_sums.1 = (f32[8,256,1024]{2,1,0:T(8,128)}, f32[128,512]{1,0:T(8,128)}) custom-call(s32[1]{0:T(128)} %bitcast.group_ref, bf16[128,512]{1,0:T(8,128)(2,1)} %mul.104.weight_ref, bf16[32,256,1024]{2,1,0:T(8,128)(2,1)} %bitcast.18, bf16[64,256,1024]{2,1,0:T(8,128)(2,1)} %maps_ref.3), custom_call_target="tpu_custom_call" | custom-call | tf_op jit(solution)/shard_map/map_sums/pallas_call | solution.py:366
  288.7 0.0 copy-start.1
  288.7 1.8 reshape.168
  290.5 0.3 multiply_reduce_fusion
  290.8 10.6 %gather_scores.1 = f32[8,4,8,128]{3,2,1,0:T(8,128)S(1)} custom-call(f32[8,128]{1,0:T(8,128)S(1)} %pad.4.in_ref), custom_call_target="tpu_custom_call" | custom-call | tf_op jit(solution)/shard_map/gather_scores/pallas_call | solution.py:655
  301.4 0.9 fusion
  302.3 0.0 copy-done.1
  (10 shorter events, 0.1 us)
Async XLA Ops:
  0.6 4.1 %copy-start = (bf16[64,64]{1,0:T(8,128)(2,1)S(1)}, bf16[64,64]{1,0:T(8,128)(2,1)}, u32[]{:S(2)}) copy-start(bf16[64,64]{1,0:T(8,128)(2,1)} %param.9) | copy-start | bytes 24580
  25.6 1.3 copy-start.2
  288.7 13.6 %copy-start.1 = (bf16[64,64]{1,0:T(8,128)(2,1)S(1)}, bf16[64,64]{1,0:T(8,128)(2,1)}, u32[]{:S(2)}) copy-start(bf16[64,64]{1,0:T(8,128)(2,1)} %param.9) | copy-start | bytes 24580
